TPU v7x, 128 devices: a whole 4x4x4 slice. The times are simulated.
128 devices in a mesh: group: 8 (over y, core), dev: 16 (over z, x).
Axes of the slice: x: 4, y: 4, z: 4, core: 2. Of those that a mesh axis runs over, the one named last changes fastest.
Arguments:
- primary_q: bfloat16 [256, 3584, 1024], P(('group', 'dev')), may hold values from -0.09375 to 0.09375
- primary_scales: bfloat16 [256, 28, 8], P(('group', 'dev')), may hold values from 0.5 to 2
- new_place: int32 [128], P(('group', 'dev')), may hold values from 0 to 255, as said below
- tokens: bfloat16 [2048, 3584], P(('group', 'dev')), may hold values from -6 to 6
- experts: int32 [2048, 8], P(('group', 'dev')), may hold values from 0 to 255, all different within a row
- replica: int32 [2048, 8], P(('group', 'dev')), may hold values from 0 to 1
- route_num: int32 [2048, 8], P(('group', 'dev')), may hold values from 1 to 16
Outputs:
- new_weights: bfloat16 [128, 3584, 1024], P(('group', 'dev'))
- new_scales: bfloat16 [128, 28, 8], P(('group', 'dev'))
- hidden_out: bfloat16 [2048, 8, 1024], P(('group', 'dev'))
- slot_load: int32 [128, 3], P(('group', 'dev'))
Inputs may be any that keep to these rules, and one draw needn't show every extreme that they name: `new_place`: the redundant slots of the 16 devices of one group hold 16 different experts, each with its primary copy on a device of that group.
All inputs are finite; a program needn't handle non-finite values.
Results may differ from a plain program's by a relative error of at most 0.0057.
Values may be sent and summed in bfloat16 or wider, within the bound.
A program may use at most 192 MiB of HBM per device.

v0:
```python
import jax
import jax.numpy as jnp
from jax import lax
from jax.sharding import PartitionSpec as P

D = 3584
FF = 1024
TILE = 128
CAP = 2


def dequantize(values, scales):
    tile_grid = values.astype(jnp.float32).reshape(D // TILE, TILE, FF // TILE, TILE)
    scaled = tile_grid * scales.astype(jnp.float32)[:, None, :, None]
    return scaled.reshape(D, FF).astype(jnp.bfloat16)


def spread_parts(values, scales, parts_count):
    holding, width_in, hidden = values.shape
    split_values = values.reshape(holding, parts_count, width_in // parts_count, hidden)
    split_scales = jnp.broadcast_to(scales[:, None], (holding, parts_count) + scales.shape[1:])
    return (split_values, split_scales)


def pick_parts(got_values, got_scales, wanted, first_dev):
    holding = got_values.shape[0]
    parts_count = got_values.shape[1]
    chosen = wanted % holding * parts_count + (wanted // holding - first_dev)
    values = got_values.reshape((holding * parts_count,) + got_values.shape[2:])[chosen]
    scales = got_scales.reshape((holding * parts_count,) + got_scales.shape[2:])[chosen]
    return (values, scales)


def per_device(primary_q, primary_scales, new_place, tokens, experts, replica, route_num):
    place_all = lax.all_gather(new_place, ("group", "dev"), axis=0, tiled=True)
    holding = primary_q.shape[0]
    parts_count = lax.axis_size("dev")
    first_dev = lax.axis_index("group") * parts_count
    wanted = lax.dynamic_slice_in_dim(place_all, first_dev, parts_count)
    split_values, split_scales = spread_parts(primary_q, primary_scales, parts_count)
    got_values, got_scales = (
        lax.all_to_all(split_values, "dev", split_axis=1, concat_axis=1, tiled=True),
        lax.all_to_all(split_scales, "dev", split_axis=1, concat_axis=1, tiled=True),
    )
    send_values, send_scales = pick_parts(got_values, got_scales, wanted, first_dev)
    back_values, back_scales = (
        lax.all_to_all(send_values, "dev", split_axis=0, concat_axis=0, tiled=True),
        lax.all_to_all(send_scales, "dev", split_axis=0, concat_axis=0, tiled=True),
    )
    new_weights = back_values.reshape((1, D, FF))
    new_scales = back_scales[0:1]
    row_count, top_count = experts.shape
    pair_count = row_count * top_count
    device_count = place_all.shape[0]
    expert_flat = experts.reshape(pair_count)
    device_ids = jnp.arange(device_count, dtype=jnp.int32)
    matched = expert_flat[:, None] == place_all[None, :]
    has_copy = jnp.any(matched, axis=1)
    holder = jnp.sum(jnp.where(matched, device_ids[None, :], 0), axis=1)
    use_copy = (replica.reshape(pair_count) == 1) & has_copy
    target = jnp.where(use_copy, holder, expert_flat // holding)
    slot_id = jnp.where(use_copy, holding, expert_flat % holding)
    pair_order = jnp.arange(pair_count)
    earlier = (target[:, None] == target[None, :]) & (pair_order[None, :] < pair_order[:, None])
    position = jnp.sum(earlier, axis=1)
    served = position < CAP
    cell_count = device_count * CAP
    cell_index = target * CAP + position
    placed = (cell_index[None, :] == jnp.arange(cell_count)[:, None]) & served[None, :]
    row_hits = jnp.any(placed.reshape(cell_count, row_count, top_count), axis=2)
    row_buffer = jnp.dot(row_hits.astype(jnp.bfloat16), tokens, preferred_element_type=jnp.float32)
    row_buffer = row_buffer.astype(jnp.bfloat16).reshape(device_count, CAP, D)
    code_values = jnp.sum(jnp.where(placed, slot_id[None, :] + 1, 0), axis=1) - 1
    code_buffer = code_values.astype(jnp.float32).astype(jnp.bfloat16).reshape(device_count, CAP)
    matrices = [dequantize(primary_q[member], primary_scales[member]) for member in range(holding)]
    matrices.append(dequantize(new_weights[0], new_scales[0]))
    joined = jnp.concatenate(matrices, axis=1)
    row_block = lax.all_to_all(
        row_buffer, ("group", "dev"), split_axis=0, concat_axis=0, tiled=True
    )
    slot_codes = lax.all_to_all(
        code_buffer, ("group", "dev"), split_axis=0, concat_axis=0, tiled=True
    )
    leading, item_count, width_in = row_block.shape
    product = jnp.dot(
        row_block.reshape(leading * item_count, width_in),
        joined,
        preferred_element_type=jnp.float32,
    )
    flat_codes = slot_codes.reshape(leading * item_count).astype(jnp.float32)
    picked = jnp.zeros((leading * item_count, FF), jnp.float32)
    tallies = []
    for member in range(holding + 1):
        chosen = flat_codes == member
        picked = picked + jnp.where(
            chosen[:, None], product[:, member * FF : (member + 1) * FF], 0.0
        )
        tallies.append(chosen.astype(jnp.float32))
    activated = jax.nn.silu(picked).astype(jnp.bfloat16).reshape(leading, item_count, FF)
    activated, tallies = (
        activated,
        jnp.stack(tallies, axis=1).reshape(leading, item_count, holding + 1),
    )
    returned = lax.all_to_all(activated, ("group", "dev"), split_axis=0, concat_axis=0, tiled=True)
    dest_hit = (target[None, :] == device_ids[:, None]) & served[None, :]
    slot_hit = slot_id[:, None] == jnp.arange(holding + 1)[None, :]
    counted = jnp.dot(
        dest_hit.astype(jnp.float32), slot_hit.astype(jnp.float32), precision=lax.Precision.HIGHEST
    )
    summed = lax.psum_scatter(counted, ("group", "dev"), scatter_dimension=0, tiled=True)
    slot_load = summed.astype(jnp.int32)
    selected = jnp.dot(
        placed.T.astype(jnp.bfloat16),
        returned.reshape(cell_count, FF),
        preferred_element_type=jnp.float32,
    )
    weight = route_num.reshape(pair_count).astype(jnp.float32) / 16.0
    hidden_out = (selected * weight[:, None]).astype(jnp.bfloat16).reshape(row_count, top_count, FF)
    return (new_weights, new_scales, hidden_out, slot_load)


def solution(mesh):
    in_specs = (
        P(("group", "dev"), None, None),
        P(("group", "dev"), None, None),
        P(("group", "dev")),
        P(("group", "dev"), None),
        P(("group", "dev"), None),
        P(("group", "dev"), None),
        P(("group", "dev"), None),
    )
    out_specs = (
        P(("group", "dev"), None, None),
        P(("group", "dev"), None, None),
        P(("group", "dev"), None, None),
        P(("group", "dev"), None),
    )
    return jax.shard_map(
        per_device, mesh=mesh, in_specs=in_specs, out_specs=out_specs, check_vma=False
    )
```

profile of v0, /device:TPU:1, one launch (start us, length us, event | category | flops | bytes accessed | tf_op | source)
XLA Modules:
  0.0 594.2 jit_solution(13034104524677342891)
XLA Ops:
  1.4 0.7 reshape.356
  2.1 8.4 %all-to-all-start.2 = ((bf16[16,2,224]{2,1,0:T(2,128)(2,1)}), bf16[16,2,224]{2,1,0:T(2,128)(2,1)S(1)}, u32[]{:S(2)}, u32[]{:S(2)}) async-start(bf16[16,2,224]{2,1,0:T(2,128)(2,1)} %reshape.356), calls=%async_computation.2 | async-start | bytes 32768 | tf_op jit(solution)/shard_map/all_to_all | solution.py:43
  11.3 66.6 %all-reduce = s32[128]{0:T(128)S(1)} all-reduce(s32[128]{0:T(128)S(1)} %dynamic-update-slice), channel_id=1, replica_groups=mesh['group'=8,'dev'=16] {'group','dev'}, use_global_device_ids=true, to_apply=%add | all-reduce | flops 128 | bytes 1024
  77.9 0.8 copy.62
  79.1 0.8 copy.61
  80.4 0.8 convert_element_type.161
  81.2 4.9 all-to-all-start.4
  86.3 1.2 gather_fusion.1
  87.4 8.4 %all-to-all-done.4 = bf16[128,1,2]{2,1,0:T(2,128)(2,1)S(1)} async-done(((bf16[128,1,2]{2,1,0:T(2,128)(2,1)}), bf16[128,1,2]{2,1,0:T(2,128)(2,1)S(1)}, u32[]{:S(2)}, u32[]{:S(2)}) %all-to-all-start.4) | async-done | bytes 544 | tf_op jit(solution)/shard_map/all_to_all | solution.py:81
  95.8 3.5 all-to-all-start.3
  99.3 13.7 %copy.58 = bf16[2,16,224,1024]{3,2,0,1:T(8,128)(2,1)} copy(bf16[2,16,224,1024]{3,2,1,0:T(8,128)(2,1)} %bitcast.49) | data formatting | bytes 29360128 | tf_op jit(solution)/shard_map/reshape | solution.py:20
  113.0 6.6 %all-to-all-start = ((bf16[2,16,224,1024]{3,2,0,1:T(8,128)(2,1)}), bf16[2,16,224,1024]{3,2,0,1:T(8,128)(2,1)}, u32[]{:S(2)}, u32[]{:S(2)}) async-start(bf16[2,16,224,1024]{3,2,0,1:T(8,128)(2,1)} %copy.58), calls=%async_computation | async-start | bytes 29360128 | tf_op jit(solution)/shard_map/all_to_all | solution.py:42
  120.8 1.7 reshape.322
  122.5 212.4 %all-to-all-done = bf16[2,16,224,1024]{3,2,0,1:T(8,128)(2,1)} async-done(((bf16[2,16,224,1024]{3,2,0,1:T(8,128)(2,1)}), bf16[2,16,224,1024]{3,2,0,1:T(8,128)(2,1)}, u32[]{:S(2)}, u32[]{:S(2)}) %all-to-all-start) | async-done | bytes 14680096 | tf_op jit(solution)/shard_map/all_to_all | solution.py:42
  334.9 7.7 %all-to-all-start.5 = ((bf16[128,2,3584]{2,1,0:T(2,128)(2,1)}), bf16[128,2,3584]{2,1,0:T(2,128)(2,1)S(1)}, u32[]{:S(2)}, u32[]{:S(2)}) async-start(bf16[128,2,3584]{2,1,0:T(2,128)(2,1)} %reshape.322), calls=%async_computation.5 | async-start | bytes 3670016 | tf_op jit(solution)/shard_map/all_to_all | solution.py:78
  342.5 13.7 %copy.59 = bf16[2,16,224,1024]{3,2,1,0:T(8,128)(2,1)} copy(bf16[2,16,224,1024]{3,2,0,1:T(8,128)(2,1)} %all-to-all-done) | data formatting | bytes 29360128 | tf_op jit(solution)/shard_map/all_to_all | solution.py:42
  356.2 9.2 %gather_fusion = bf16[16,224,1024]{2,1,0:T(8,128)(2,1)} fusion(bf16[32,224,1024]{2,1,0:T(8,128)(2,1)} %bitcast.53, s32[1024]{0:T(1024)S(1)} %pad_clamp_fusion), kind=kCustom, calls=%fused_computation | custom fusion | bytes 14680128 | tf_op jit(solution)/shard_map/gather | solution.py:29
  365.5 3.9 all-to-all-done.5
  369.4 4.9 all-to-all-start.1
  374.5 1.0 mul.65
  375.5 6.2 %mul.68 = f32[28,128,8,128]{3,2,1,0:T(8,128)} broadcast(f32[28,8]{1,0:T(8,128)S(1)} %copy.69), dimensions={0,2} | broadcast | bytes 14680960 | tf_op jit(solution)/shard_map/mul | solution.py:14
  381.7 18.6 %fusion.8 = (bf16[3584,1024]{1,0:T(8,128)(2,1)}, bf16[3584,1024]{1,0:T(8,128)(2,1)}) fusion(f32[448,8,8,128]{3,2,1,0:T(8,128)S(1)} %bitcast.50, bf16[2,3584,1024]{2,1,0:T(8,128)(2,1)} %param.7, f32[448,8,8,128]{3,2,1,0:T(8,128)} %bitcast.51), kind=kLoop, calls=%fused_computation.13 | loop fusion | flops 22020096 | bytes 58720256 | tf_op jit(solution)/shard_map/convert_element_type | solution.py:15
  402.1 1.7 reshape.323
  403.8 77.2 %all-to-all-done.1 = bf16[16,224,1024]{2,1,0:T(8,128)(2,1)} async-done(((bf16[16,224,1024]{2,1,0:T(8,128)(2,1)}), bf16[16,224,1024]{2,1,0:T(8,128)(2,1)}, u32[]{:S(2)}, u32[]{:S(2)}) %all-to-all-start.1) | async-done | bytes 7340064 | tf_op jit(solution)/shard_map/all_to_all | solution.py:47
  480.9 1.0 mul.71
  482.0 9.2 %fusion.6 = bf16[3584,1024]{1,0:T(8,128)(2,1)} fusion(f32[448,8,8,128]{3,2,1,0:T(8,128)S(1)} %bitcast.52, bf16[16,224,1024]{2,1,0:T(8,128)(2,1)} %all-to-all-done.1), kind=kLoop, calls=%fused_computation.9 | loop fusion | flops 11010048 | bytes 29360128 | tf_op jit(solution)/shard_map/convert_element_type | solution.py:15
  491.2 15.5 %fusion = f32[256,3072]{1,0:T(8,128)S(1)} fusion(bf16[256,3584]{1,0:T(8,128)(2,1)S(1)} %copy-done.2, bf16[3584,1024]{1,0:T(8,128)(2,1)} %fusion.6, bf16[3584,1024]{1,0:T(8,128)(2,1)} %get-tuple-element.12, bf16[3584,1024]{1,0:T(8,128)(2,1)S(1)} %bitcast.55), kind=kOutput, calls=%fused_computation.2 | convolution fusion | flops 5703204864 | bytes 27000832 | tf_op jit(solution)/shard_map/dot_general | solution.py:85
  507.2 1.0 reshape.324
  508.2 9.2 %all-to-all-start.6 = ((bf16[128,2,1024]{2,1,0:T(2,128)(2,1)}), bf16[128,2,1024]{2,1,0:T(2,128)(2,1)S(1)}, u32[]{:S(2)}, u32[]{:S(2)}) async-start(bf16[128,2,1024]{2,1,0:T(2,128)(2,1)} %reshape.324), calls=%async_computation.6 | async-start | bytes 1048576 | tf_op jit(solution)/shard_map/all_to_all | solution.py:104
  517.8 67.6 %all-reduce.1 = f32[128,3]{1,0:T(8,128)S(1)} all-reduce(f32[128,3]{1,0:T(8,128)S(1)} %fusion.21), channel_id=2, replica_groups=mesh['group'=8,'dev'=16] {'group','dev'}, use_global_device_ids=true, to_apply=%region_5.6.clone | all-reduce | flops 384 | bytes 3072
  586.2 1.0 fusion.10
  587.1 7.0 %copy.81 = bf16[1,3584,1024]{2,1,0:T(8,128)(2,1)} copy(bf16[1,3584,1024]{2,1,0:T(8,128)(2,1)} %bitcast.2) | data formatting | bytes 14680064
  (59 shorter events, 6.5 us)
Async XLA Ops:
  0.6 119.5 %copy-start = (bf16[16,3584]{1,0:T(8,128)(2,1)S(1)}, bf16[16,3584]{1,0:T(8,128)(2,1)}, u32[]{:S(2)}) copy-start(bf16[16,3584]{1,0:T(8,128)(2,1)} %param.10) | copy-start | bytes 344068
  2.1 79.1 %all-to-all-start.2 = ((bf16[16,2,224]{2,1,0:T(2,128)(2,1)}), bf16[16,2,224]{2,1,0:T(2,128)(2,1)S(1)}, u32[]{:S(2)}, u32[]{:S(2)}) async-start(bf16[16,2,224]{2,1,0:T(2,128)(2,1)} %reshape.356), calls=%async_computation.2 | async-start | bytes 32768 | tf_op jit(solution)/shard_map/all_to_all | solution.py:43
  81.2 14.6 %all-to-all-start.4 = ((bf16[128,1,2]{2,1,0:T(2,128)(2,1)}), bf16[128,1,2]{2,1,0:T(2,128)(2,1)S(1)}, u32[]{:S(2)}, u32[]{:S(2)}) async-start(bf16[128,1,2]{2,1,0:T(2,128)(2,1)} %convert_element_type.161), calls=%async_computation.4 | async-start | bytes 131072 | tf_op jit(solution)/shard_map/all_to_all | solution.py:81
  95.8 17.2 %all-to-all-start.3 = ((bf16[16,28,8]{1,2,0:T(8,128)(2,1)}), bf16[16,28,8]{1,2,0:T(8,128)(2,1)S(1)}, u32[]{:S(2)}, u32[]{:S(2)}) async-start(bf16[16,28,8]{1,2,0:T(8,128)(2,1)} %gather_fusion.1), calls=%async_computation.3 | async-start | bytes 65536 | tf_op jit(solution)/shard_map/all_to_all | solution.py:48
  113.0 221.8 %all-to-all-start = ((bf16[2,16,224,1024]{3,2,0,1:T(8,128)(2,1)}), bf16[2,16,224,1024]{3,2,0,1:T(8,128)(2,1)}, u32[]{:S(2)}, u32[]{:S(2)}) async-start(bf16[2,16,224,1024]{3,2,0,1:T(8,128)(2,1)} %copy.58), calls=%async_computation | async-start | bytes 29360128 | tf_op jit(solution)/shard_map/all_to_all | solution.py:42
  334.9 34.5 %all-to-all-start.5 = ((bf16[128,2,3584]{2,1,0:T(2,128)(2,1)}), bf16[128,2,3584]{2,1,0:T(2,128)(2,1)S(1)}, u32[]{:S(2)}, u32[]{:S(2)}) async-start(bf16[128,2,3584]{2,1,0:T(2,128)(2,1)} %reshape.322), calls=%async_computation.5 | async-start | bytes 3670016 | tf_op jit(solution)/shard_map/all_to_all | solution.py:78
  365.5 8.8 %copy-start.3 = (bf16[2,28,8]{1,2,0:T(8,128)(2,1)S(1)}, bf16[2,28,8]{1,2,0:T(8,128)(2,1)}, u32[]{:S(2)}) copy-start(bf16[2,28,8]{1,2,0:T(8,128)(2,1)} %param.8) | copy-start | bytes 2692
  369.4 111.5 %all-to-all-start.1 = ((bf16[16,224,1024]{2,1,0:T(8,128)(2,1)}), bf16[16,224,1024]{2,1,0:T(8,128)(2,1)}, u32[]{:S(2)}, u32[]{:S(2)}) async-start(bf16[16,224,1024]{2,1,0:T(8,128)(2,1)} %gather_fusion), calls=%async_computation.1 | async-start | bytes 14680064 | tf_op jit(solution)/shard_map/all_to_all | solution.py:47
  480.9 10.3 %slice-start = ((s8[7340032]{0:T(1024)(128)(4,1)}), s8[4194304]{0:T(1024)(128)(4,1)S(1)}, s32[]{:S(2)}) async-start(s8[7340032]{0:T(1024)(128)(4,1)} %bitcast.54), calls=%async_computation.7 | async-start | bytes 8388608
  481.9 9.3 %slice-start.1 = ((s8[7340032]{0:T(1024)(128)(4,1)}), s8[3145728]{0:T(1024)(128)(4,1)S(1)}, s32[]{:S(2)}) async-start(s8[7340032]{0:T(1024)(128)(4,1)} %bitcast.54), calls=%async_computation.8 | async-start | bytes 6291456
  481.9 9.3 %copy-start.2 = (bf16[256,3584]{1,0:T(8,128)(2,1)S(1)}, bf16[256,3584]{1,0:T(8,128)(2,1)}, u32[]{:S(2)}) copy-start(bf16[256,3584]{1,0:T(8,128)(2,1)} %reshape.323) | copy-start | bytes 5505028
  491.2 26.2 %copy-start.4 = (s32[16,8]{0,1:T(8,128)S(1)}, s32[16,8]{0,1:T(8,128)}, u32[]{:S(2)}) copy-start(s32[16,8]{0,1:T(8,128)} %param.13) | copy-start | bytes 1540
  508.2 77.7 %all-to-all-start.6 = ((bf16[128,2,1024]{2,1,0:T(2,128)(2,1)}), bf16[128,2,1024]{2,1,0:T(2,128)(2,1)S(1)}, u32[]{:S(2)}, u32[]{:S(2)}) async-start(bf16[128,2,1024]{2,1,0:T(2,128)(2,1)} %reshape.324), calls=%async_computation.6 | async-start | bytes 1048576 | tf_op jit(solution)/shard_map/all_to_all | solution.py:104
  587.1 7.0 %copy-start.1 = (bf16[16,3584]{1,0:T(8,128)(2,1)S(1)}, bf16[16,3584]{1,0:T(8,128)(2,1)}, u32[]{:S(2)}) copy-start(bf16[16,3584]{1,0:T(8,128)(2,1)} %param.10) | copy-start | bytes 344068
where the time goes:
time: 595 us; the launch traced here: 594 us
  waiting for transfers between devices  302 us (51%)
  blocking collectives  134 us (23%)
  local copies, waits for them, and re-layouts  63 us (11%)
  starting transfers between devices  45.2 us (8%)
  other arithmetic  31 us (5%)
  matrix products  17.4 us (3%)
    all_to_all x1, waiting for transfers between devices, per_device(): lax.all_to_all(split_values, 'dev', split_axis=1, concat_axis=1, tiled=True)  212 us
    unnamed x2, blocking collectives  134 us
    all_to_all x1, waiting for transfers between devices, per_device(): lax.all_to_all(send_values, 'dev', split_axis=0, concat_axis=0, tiled=True)  77.2 us
    convert_element_type x2, other arithmetic, dequantize(): return scaled.reshape(D, FF).astype(jnp.bfloat16)  27.9 us
    dot_general x1, matrix products, per_device(): jnp.dot(row_block.reshape(leading * item_count, width_in), joined, prefer...  15.5 us
    reshape x1, local copies, waits for them, and re-layouts, spread_parts(): values.reshape(holding, parts_count, width_in // parts_count, hidden)  13.7 us
    all_to_all x1, local copies, waits for them, and re-layouts, per_device(): lax.all_to_all(split_values, 'dev', split_axis=1, concat_axis=1, tiled=True)  13.7 us
  transfers between devices with their start and end apart: 7, of which 4 were waited for; matrix products, arithmetic and copies ran while one was open for 13% of the time, Pallas kernels for 0%

commit v1 on v0

v1 whole, which is shorter than its diff:
```python
import jax
import jax.numpy as jnp
from jax import lax
from jax.experimental import pallas as pl
from jax.experimental.pallas import tpu as pltpu
from jax.sharding import PartitionSpec as P

D = 3584
FF = 1024
TILE = 128
CAP = 2
HOLD = 2
NG = 8
ND = 16
N = NG * ND
ROWS = 16
TOPK = 8
PAIRS = ROWS * TOPK
CELLS = N * CAP
KT = D // TILE
WIDE = D + 128
BF = jnp.bfloat16
F32 = jnp.float32
I32 = jnp.int32
MESH = pl.DeviceIdType.MESH

ORDER = (
    (0, 1), (0, 3), (1, 0), (3, 0), (1, 1), (3, 3), (1, 3), (3, 1),
    (0, 2), (2, 0), (2, 2), (1, 2), (3, 2), (2, 1), (2, 3),
)
CHUNKS = ((2048, 96), (0, 128))
SUB = 16
QROWS = 512


def iota(shape, dim):
    return lax.broadcasted_iota(I32, shape, dim)


def unpack_rows(flat, blocks):
    @pl.loop(0, CELLS // 8)
    def _(i):
        v = flat[pl.ds(pl.multiple_of(8 * i, 8), 8), :]
        for j in range(4):
            blocks[4 * i + j] = v[2 * j : 2 * j + 2].astype(BF)


def pack_rows(blocks, flat):
    @pl.loop(0, CELLS // 8)
    def _(i):
        v = [blocks[4 * i + j].astype(F32) for j in range(4)]
        flat[pl.ds(pl.multiple_of(8 * i, 8), 8), :] = jnp.concatenate(v, axis=0)


def kernel(
    q, scales, place, tokens, experts, replica, route,
    w_out, scale_out, hidden_out, load_out,
    place_tx, place_rx, place_sm, meta_tx, meta_rx,
    relay_a, relay_b, send_a, send_b, w_new,
    big, tx, rx, xm, acc, back_tx, back_rx, qbuf, grow, placed_t,
    sem_place, sem_meta, sem_p1s, sem_p1r, sem_p2s, sem_p2r,
    sem_tok, sem_ret, sem_local, sem_q, sem_w,
):
    g = lax.axis_index("group")
    d = lax.axis_index("dev")
    z, x = d // 4, d % 4
    me = g * ND + d

    def peer(o):
        return lax.rem(z + o[0], 4) * 4 + lax.rem(x + o[1], 4)

    def everyone(off):
        t = lax.rem(me + off, N)
        return t, (t // ND, lax.rem(t, ND))

    def remote(src, dst, ssem, rsem, dev):
        return pltpu.make_async_remote_copy(
            src_ref=src, dst_ref=dst, send_sem=ssem, recv_sem=rsem,
            device_id=dev, device_id_type=MESH,
        )

    place_tx[...] = jnp.full((1, 128), place[0], I32)
    place_rx[me] = jnp.full((1, 128), place[0], I32)
    spread = jnp.zeros((KT, 128), F32)
    for m in range(HOLD):
        pick = (iota((8, 128), 1) == iota((8, 128), 0) + 8 * m).astype(BF)
        spread += jnp.dot(scales[m], pick, preferred_element_type=F32)
    meta_tx[0:KT] = spread.astype(BF)
    meta_tx[KT:] = jnp.zeros((32 - KT, 128), BF)

    barrier = pltpu.get_barrier_semaphore()

    @pl.loop(1, N)
    def _(off):
        _, dev = everyone(off)
        pl.semaphore_signal(barrier, inc=1, device_id=dev, device_id_type=MESH)

    pl.semaphore_wait(barrier, N - 1)

    @pl.loop(1, N)
    def _(off):
        _, dev = everyone(off)
        remote(place_tx, place_rx.at[me], sem_place.at[0], sem_place.at[1], dev).start()

    for o in ORDER:
        remote(meta_tx, meta_rx.at[d], sem_meta.at[0], sem_meta.at[1], (g, peer(o))).start()
    meta_own = pltpu.make_async_copy(meta_tx, meta_rx.at[d], sem_local.at[0])
    meta_own.start()

    relays = (relay_a, relay_b)
    sends = (send_a, send_b)
    own = []
    for c, (base, rows) in enumerate(CHUNKS):
        @pl.loop(0, rows // SUB)
        def _(s, c=c, base=base, rows=rows):
            for o in ORDER:
                p = peer(o)
                remote(
                    q.at[:, pl.ds(pl.multiple_of(base + p * rows + s * SUB, SUB), SUB)],
                    relays[c].at[d, :, pl.ds(pl.multiple_of(s * SUB, SUB), SUB)],
                    sem_p1s.at[c], sem_p1r.at[c], (g, p),
                ).start()
        cp = pltpu.make_async_copy(
            q.at[:, pl.ds(pl.multiple_of(base + d * rows, SUB), rows)], relays[c].at[d], sem_local.at[1 + c]
        )
        cp.start()
        own.append(cp)

    def q_copy(i):
        return pltpu.make_async_copy(
            q.at[i // (D // QROWS), pl.ds(pl.multiple_of(lax.rem(i, D // QROWS) * QROWS, QROWS), QROWS)],
            qbuf.at[lax.rem(i, 2)], sem_q.at[lax.rem(i, 2)],
        )

    q_copy(0).start()

    def to_row(a):
        rep = (lax.rem(iota((TOPK, PAIRS), 1), TOPK) == iota((TOPK, PAIRS), 0)).astype(BF)
        wide = jnp.dot(a[...].astype(F32).astype(BF), rep, preferred_element_type=F32)
        mine = iota((ROWS, PAIRS), 1) // TOPK == iota((ROWS, PAIRS), 0)
        return jnp.sum(jnp.where(mine, wide, 0.0), axis=0, keepdims=True)

    def to_col(row):
        return jnp.broadcast_to(row, (PAIRS, PAIRS)).T

    expert_row = to_row(experts)
    replica_row = to_row(replica)
    weight_col = to_col(to_row(route) * (1.0 / 16.0))

    def wait_recv_all(ref, sem):
        pltpu.make_async_copy(ref, ref, sem).wait()

    wait_recv_all(place_rx.at[pl.ds(0, N - 1)], sem_place.at[1])
    sm = pltpu.make_async_copy(place_rx.at[pl.ds(pl.multiple_of(g * ND, ND), ND)], place_sm, sem_local.at[3])
    sm.start()

    hold_of = place_rx[...].reshape(N, 128).astype(F32)
    match = hold_of == expert_row
    dev_ids = iota((N, PAIRS), 0).astype(F32)
    holder = jnp.sum(jnp.where(match, dev_ids, 0.0), axis=0, keepdims=True)
    found = jnp.sum(jnp.where(match, 1.0, 0.0), axis=0, keepdims=True)
    use_copy = (replica_row > 0.5) & (found > 0.5)
    home = jnp.floor(expert_row * 0.5)
    target = jnp.where(use_copy, holder, home)
    slot = jnp.where(use_copy, float(HOLD), expert_row - 2.0 * home)
    target_col = to_col(target)
    slot_col = to_col(slot)
    earlier = (target_col == target) & (iota((PAIRS, PAIRS), 0) < iota((PAIRS, PAIRS), 1))
    position = jnp.sum(jnp.where(earlier, 1.0, 0.0), axis=0, keepdims=True)
    cell = jnp.where(position < CAP, target * CAP + position, -1.0)
    placed = jnp.where(iota((CELLS, PAIRS), 0).astype(F32) == cell, 1.0, 0.0)
    cell_col = jnp.concatenate([to_col(cell)] * 2, axis=1)
    placed_t[...] = jnp.where(iota((PAIRS, CELLS), 1).astype(F32) == cell_col, 1.0, 0.0).astype(BF)
    placed = placed.astype(BF)
    to_rows = (iota((PAIRS, ROWS), 0) // TOPK == iota((PAIRS, ROWS), 1)).astype(BF)
    row_pick = jnp.dot(placed, to_rows, preferred_element_type=F32).astype(BF)

    @pl.loop(0, D // 512)
    def _(i):
        cols = pl.ds(pl.multiple_of(i * 512, 512), 512)
        big[:, cols] = jnp.dot(row_pick, tokens[:, cols], preferred_element_type=F32)

    big[:, D:] = jnp.dot(placed, (slot_col + 1.0).astype(BF), preferred_element_type=F32) - 1.0

    unpack_rows(big, tx)

    @pl.loop(1, N)
    def _(off):
        t, dev = everyone(off)
        remote(tx.at[t], rx.at[me], sem_tok.at[0], sem_tok.at[1], dev).start()

    tok_own = pltpu.make_async_copy(tx.at[me], rx.at[me], sem_local.at[4])
    tok_own.start()

    sm.wait()

    def relay_select(c):
        base, rows = CHUNKS[c]
        own[c].wait()
        wait_recv_all(relays[c].at[pl.ds(0, ND - 1)], sem_p1r.at[c])

        @pl.loop(0, ND)
        def _(p):
            w = place_sm[p, 0, 0]
            sends[c][p] = relays[c][lax.rem(w // HOLD, ND), lax.rem(w, HOLD)]

        mine = pl.ds(pl.multiple_of(base + d * rows, SUB), rows)
        for i, o in enumerate(ORDER):
            p = peer(o)
            remote(sends[c].at[p], w_new.at[mine], sem_p2s.at[c], sem_p2r.at[i, c], (g, p)).start()
        pltpu.make_async_copy(sends[c].at[d], w_new.at[mine], sem_local.at[5 + c]).start()

    relay_select(0)
    relay_select(1)

    meta_own.wait()
    wait_recv_all(meta_rx.at[pl.ds(0, ND - 1)], sem_meta.at[1])
    mine_w = place[0]
    got = meta_rx[lax.rem(mine_w // HOLD, ND)]
    slot_m = lax.rem(mine_w, HOLD)
    keep = (iota((128, 128), 0) == iota((128, 128), 1) + 8 * slot_m).astype(BF)
    scale_out[...] = jnp.dot(got, keep, preferred_element_type=F32).astype(BF)

    def grow_scales(block, m):
        sel = (iota((128, FF), 0) == iota((128, FF), 1) // TILE + 8 * m).astype(BF)
        return jnp.dot(block, sel, preferred_element_type=F32).reshape(32, 1, FF)

    for m in range(HOLD):
        grow[m] = grow_scales(meta_tx[...], m)
    grow[HOLD] = grow_scales(got, slot_m)

    tok_own.wait()
    wait_recv_all(rx.at[pl.ds(0, N - 1)], sem_tok.at[1])

    pack_rows(rx, big)

    code = big[:, D:]
    load_row = jnp.zeros((1, 128), F32)
    for s in range(HOLD + 1):
        count = jnp.sum(jnp.where(code == float(s), 1.0, 0.0), axis=0, keepdims=True)
        load_row = jnp.where(iota((1, 128), 1) == s, count, load_row)
    load_out[...] = jnp.broadcast_to(load_row, (8, 128)).astype(I32)

    for s in range(HOLD + 1):
        @pl.loop(0, KT)
        def _(k, s=s):
            cols = pl.ds(pl.multiple_of(k * TILE, TILE), TILE)
            xm[s, :, cols] = jnp.where(code == float(s), big[:, cols], 0.0).astype(BF)

    acc[...] = jnp.zeros((CELLS, FF), F32)
    n_q = HOLD * (D // QROWS)

    @pl.loop(0, n_q)
    def _(i):
        @pl.when(i + 1 < n_q)
        def _():
            q_copy(i + 1).start()
        q_copy(i).wait()
        m = i // (D // QROWS)
        tile0 = lax.rem(i, D // QROWS) * (QROWS // TILE)
        w = qbuf[lax.rem(i, 2)].astype(F32).reshape(QROWS // TILE, TILE, FF)
        w = (w * grow[m, pl.ds(tile0, QROWS // TILE)]).astype(BF).reshape(QROWS, FF)
        xs = xm[m, :, pl.ds(pl.multiple_of(tile0 * TILE, TILE), QROWS)]
        acc[...] += jnp.dot(xs, w, preferred_element_type=F32)

    def w_tile(k, n):
        rows = pl.ds(pl.multiple_of(k * TILE, TILE), n * TILE)
        w = w_new[rows].astype(F32).reshape(n, TILE, FF)
        w = (w * grow[HOLD, pl.ds(k, n)]).astype(BF).reshape(n * TILE, FF)
        acc[...] += jnp.dot(xm[HOLD, :, rows], w, preferred_element_type=F32)

    def w_wait(i, c):
        base, rows = CHUNKS[c]
        ref = w_new.at[pl.ds(base, rows)]
        pltpu.make_async_copy(ref, ref, sem_p2r.at[i, c]).wait()

    def w_own(c):
        base, rows = CHUNKS[c]
        mine = pl.ds(pl.multiple_of(base + d * rows, SUB), rows)
        pltpu.make_async_copy(sends[c].at[d], w_new.at[mine], sem_local.at[5 + c]).wait()

    w_own(0)
    for i in range(len(ORDER)):
        w_wait(i, 0)
    out_a = pltpu.make_async_copy(w_new.at[pl.ds(2048, 1536)], w_out.at[pl.ds(2048, 1536)], sem_w.at[0])
    out_a.start()

    @pl.loop(0, 3)
    def _(i):
        w_tile(16 + 4 * i, 4)

    w_own(1)
    w_tile(d, 1)
    for i, o in enumerate(ORDER):
        w_wait(i, 1)
        k = lax.rem(z + 4 - o[0], 4) * 4 + lax.rem(x + 4 - o[1], 4)
        w_tile(k, 1)
    out_b = pltpu.make_async_copy(w_new.at[pl.ds(0, 2048)], w_out.at[pl.ds(0, 2048)], sem_w.at[1])
    out_b.start()

    v = acc[...]
    acc[...] = v / (1.0 + jnp.exp(-v))

    unpack_rows(acc, back_tx)

    @pl.loop(1, N)
    def _(off):
        t, dev = everyone(off)
        remote(back_tx.at[t], back_rx.at[me], sem_ret.at[0], sem_ret.at[1], dev).start()

    ret_own = pltpu.make_async_copy(back_tx.at[me], back_rx.at[me], sem_local.at[7])
    ret_own.start()
    ret_own.wait()
    wait_recv_all(back_rx.at[pl.ds(0, N - 1)], sem_ret.at[1])

    pack_rows(back_rx, acc)

    selected = jnp.dot(placed_t[...], acc[...].astype(BF), preferred_element_type=F32)
    hidden_out[...] = (selected * weight_col[:, 0:1]).astype(BF)

    wait_recv_all(place_rx.at[pl.ds(0, N - 1)], sem_place.at[0])
    wait_recv_all(meta_rx.at[pl.ds(0, ND - 1)], sem_meta.at[0])
    for c in range(2):
        wait_recv_all(relays[c].at[pl.ds(0, ND - 1)], sem_p1s.at[c])
        wait_recv_all(sends[c].at[pl.ds(0, ND - 1)], sem_p2s.at[c])
    wait_recv_all(tx.at[pl.ds(0, N - 1)], sem_tok.at[0])
    wait_recv_all(back_tx.at[pl.ds(0, N - 1)], sem_ret.at[0])
    out_a.wait()
    out_b.wait()


def per_device(primary_q, primary_scales, new_place, tokens, experts, replica, route_num):
    vmem = pl.BlockSpec(memory_space=pltpu.VMEM)
    anywhere = pl.BlockSpec(memory_space=pl.ANY)
    dma = pltpu.SemaphoreType.DMA
    scratch = [
        pltpu.VMEM((1, 128), I32),
        pltpu.VMEM((N, 1, 128), I32),
        pltpu.SMEM((ND, 1, 128), I32),
        pltpu.VMEM((32, 128), BF),
        pltpu.VMEM((ND, 32, 128), BF),
        pltpu.VMEM((ND, HOLD, CHUNKS[0][1], FF), BF),
        pltpu.VMEM((ND, HOLD, CHUNKS[1][1], FF), BF),
        pltpu.VMEM((ND, CHUNKS[0][1], FF), BF),
        pltpu.VMEM((ND, CHUNKS[1][1], FF), BF),
        pltpu.VMEM((D, FF), BF),
        pltpu.VMEM((CELLS, WIDE), F32),
        pltpu.VMEM((N, CAP, WIDE), BF),
        pltpu.VMEM((N, CAP, WIDE), BF),
        pltpu.VMEM((HOLD + 1, CELLS, D), BF),
        pltpu.VMEM((CELLS, FF), F32),
        pltpu.VMEM((N, CAP, FF), BF),
        pltpu.VMEM((N, CAP, FF), BF),
        pltpu.VMEM((2, QROWS, FF), BF),
        pltpu.VMEM((HOLD + 1, 32, 1, FF), F32),
        pltpu.VMEM((PAIRS, CELLS), BF),
        dma((2,)), dma((2,)), dma((2,)), dma((2,)), dma((2,)), dma((len(ORDER), 2)),
        dma((2,)), dma((2,)), dma((8,)), dma((2,)), dma((2,)),
    ]
    new_weights, scale_tile, hidden, load = pl.pallas_call(
        kernel,
        out_shape=(
            jax.ShapeDtypeStruct((D, FF), BF),
            jax.ShapeDtypeStruct((32, 128), BF),
            jax.ShapeDtypeStruct((PAIRS, FF), BF),
            jax.ShapeDtypeStruct((8, 128), I32),
        ),
        in_specs=[
            anywhere, vmem, pl.BlockSpec(memory_space=pltpu.SMEM), vmem, vmem, vmem, vmem,
        ],
        out_specs=(anywhere, vmem, vmem, vmem),
        scratch_shapes=scratch,
        compiler_params=pltpu.CompilerParams(
            collective_id=0, has_side_effects=True, vmem_limit_bytes=64000 * 1024
        ),
    )(primary_q, primary_scales, new_place, tokens, experts, replica, route_num)
    return (
        new_weights.reshape(1, D, FF),
        scale_tile[:KT, :8].reshape(1, KT, 8),
        hidden.reshape(ROWS, TOPK, FF),
        load[0:1, : HOLD + 1],
    )


def solution(mesh):
    both = ("group", "dev")
    return jax.shard_map(
        per_device,
        mesh=mesh,
        in_specs=(
            P(both, None, None), P(both, None, None), P(both), P(both, None),
            P(both, None), P(both, None), P(both, None),
        ),
        out_specs=(P(both, None, None), P(both, None, None), P(both, None, None), P(both, None)),
        check_vma=False,
    )
```

time: 595 us -> 354 us (0.59)
  Pallas kernels: 0 us -> 337 us
  waiting for transfers between devices: 302 us -> 0 us
  blocking collectives: 134 us -> 0 us
  local copies, waits for them, and re-layouts: 63 us -> 15.7 us
  starting transfers between devices: 45.2 us -> 0 us
  other arithmetic: 31 us -> 0 us
  matrix products: 17.4 us -> 0 us
    pallas_call x0 -> x1, Pallas kernels: none -> 337 us  [per_device(): pl.pallas_call(kernel, out_shape=(jax.ShapeDtypeStruct((D, FF), BF), jax....]
    all_to_all x7 -> x0, waiting for transfers between devices: 302 us -> none  [the longest x1 212 us: per_device(): lax.all_to_all(split_values, 'dev', split_axis=1, concat_axis=1, tiled=True)]
    unnamed x2 -> x0, blocking collectives: 134 us -> none
    all_to_all x7 -> x0, starting transfers between devices: 45.2 us -> none  [the longest x1 9.21 us: per_device(): lax.all_to_all(activated, ('group', 'dev'), split_axis=0, concat_axis=0,...]
    convert_element_type x7 -> x0, other arithmetic: 29.4 us -> none  [the longest x2 27.9 us: dequantize(): return scaled.reshape(D, FF).astype(jnp.bfloat16)]
    reshape x5 -> x1, local copies, waits for them, and re-layouts: 18.2 us -> 0.7 us  [per_device(): scale_tile[:KT, :8].reshape(1, KT, 8)]
    dot_general x4 -> x0, matrix products: 17.4 us -> none  [the longest x1 15.5 us: per_device(): jnp.dot(row_block.reshape(leading * item_count, width_in), joined, prefer...]
    all_to_all x2 -> x0, local copies, waits for them, and re-layouts: 13.7 us -> none  [the longest x1 13.7 us: per_device(): lax.all_to_all(split_values, 'dev', split_axis=1, concat_axis=1, tiled=True)]
  transfers between devices with their start and end apart: 7 -> 0, of which waited for: 4 -> 0; matrix products, arithmetic and copies ran while one was open for 13% -> 0% of each run, Pallas kernels for 0% -> 0%
where the time goes in v1:
time: 354 us
  Pallas kernels  337 us (95%)
  local copies, waits for them, and re-layouts  15.7 us (4%)
    pallas_call x1, Pallas kernels, per_device(): pl.pallas_call(kernel, out_shape=(jax.ShapeDtypeStruct((D, FF), BF), jax....  337 us
    unnamed x9, local copies, waits for them, and re-layouts  13.8 us

profile of v1, /device:TPU:1, one launch (start us, length us, event | category | flops | bytes accessed | tf_op | source)
XLA Modules:
  0.0 353.6 jit_solution(18119942255665444326)
XLA Ops:
  1.3 1.4 copy.12.experts
  2.6 1.4 copy.13.replica
  4.0 1.3 copy.14.route
  5.3 1.4 copy.11.scales
  6.7 336.6 %shard_map.102 = (bf16[3584,1024]{1,0:T(8,128)(2,1)}, bf16[32,128]{1,0:T(8,128)(2,1)}, bf16[128,1024]{1,0:T(8,128)(2,1)}, s32[8,128]{1,0:T(8,128)}) custom-call(bf16[2,3584,1024]{2,1,0:T(8,128)(2,1)} %q.1, bf16[2,28,8]{2,1,0:T(8,128)(2,1)} %copy.11.scales, s32[1]{0:T(128)S(6)} %copy.18.place, bf16[16,3584]{1,0:T(8,128)(2,1)} %tokens.1, ...), custom_call_target="tpu_custom_call" | custom-call | tf_op jit(solution)/shard_map/pallas_call | solution.py:360
  343.3 1.2 slice.7
  344.5 0.7 slice_bitcast_fusion
  345.2 0.7 copy.15
  345.9 0.0 copy-start
  345.9 7.0 %copy.19 = bf16[1,3584,1024]{2,1,0:T(8,128)(2,1)} copy(bf16[1,3584,1024]{2,1,0:T(8,128)(2,1)} %bitcast.4) | data formatting | bytes 14680064
  352.9 0.0 copy-done
  352.9 0.7 copy.20
Async XLA Ops:
  345.9 7.0 %copy-start = (bf16[128,1024]{1,0:T(8,128)(2,1)S(1)}, bf16[128,1024]{1,0:T(8,128)(2,1)}, u32[]{:S(2)}) copy-start(bf16[128,1024]{1,0:T(8,128)(2,1)} %get-tuple-element.10) | copy-start | bytes 786436

commit v2 on v1

--- a/solution.py
+++ b/solution.py
@@ -30,6 +30,7 @@
 )
 CHUNKS = ((2048, 96), (0, 128))
 SUB = 16
+EARLY = 3
 QROWS = 512
 
 
@@ -45,10 +46,11 @@
             blocks[4 * i + j] = v[2 * j : 2 * j + 2].astype(BF)
 
 
-def pack_rows(blocks, flat):
+def pack_rows(blocks, flat, nested=False):
     @pl.loop(0, CELLS // 8)
     def _(i):
-        v = [blocks[4 * i + j].astype(F32) for j in range(4)]
+        at = [(i // 2, lax.rem(i, 2) * 4 + j) if nested else (4 * i + j,) for j in range(4)]
+        v = [blocks[a].astype(F32) for a in at]
         flat[pl.ds(pl.multiple_of(8 * i, 8), 8), :] = jnp.concatenate(v, axis=0)
 
 
@@ -57,9 +59,9 @@
     w_out, scale_out, hidden_out, load_out,
     place_tx, place_rx, place_sm, meta_tx, meta_rx,
     relay_a, relay_b, send_a, send_b, w_new,
-    big, tx, rx, xm, acc, back_tx, back_rx, qbuf, grow, placed_t,
-    sem_place, sem_meta, sem_p1s, sem_p1r, sem_p2s, sem_p2r,
-    sem_tok, sem_ret, sem_local, sem_q, sem_w,
+    big, tx, mid, rx, xm, acc, back_tx, back_mid, back_rx, qbuf, grow, placed_t,
+    sem_place, sem_spread, sem_meta, sem_p1s, sem_p1r, sem_p2s, sem_p2r,
+    sem_tok, sem_tok2, sem_ret, sem_ret2, sem_local, sem_q, sem_w,
 ):
     g = lax.axis_index("group")
     d = lax.axis_index("dev")
@@ -69,39 +71,31 @@
     def peer(o):
         return lax.rem(z + o[0], 4) * 4 + lax.rem(x + o[1], 4)
 
-    def everyone(off):
-        t = lax.rem(me + off, N)
-        return t, (t // ND, lax.rem(t, ND))
-
     def remote(src, dst, ssem, rsem, dev):
         return pltpu.make_async_remote_copy(
             src_ref=src, dst_ref=dst, send_sem=ssem, recv_sem=rsem,
             device_id=dev, device_id_type=MESH,
         )
 
+    def across(i):
+        return lax.rem(g + i, NG)
+
     place_tx[...] = jnp.full((1, 128), place[0], I32)
     place_rx[me] = jnp.full((1, 128), place[0], I32)
-    spread = jnp.zeros((KT, 128), F32)
-    for m in range(HOLD):
-        pick = (iota((8, 128), 1) == iota((8, 128), 0) + 8 * m).astype(BF)
-        spread += jnp.dot(scales[m], pick, preferred_element_type=F32)
-    meta_tx[0:KT] = spread.astype(BF)
-    meta_tx[KT:] = jnp.zeros((32 - KT, 128), BF)
+    widen = (iota((KT, 128), 0) == iota((KT, 128), 1)).astype(BF)
+    spread = [jnp.dot(scales[m], widen, preferred_element_type=F32) for m in range(HOLD)]
+    meta_tx[...] = jnp.concatenate(spread, axis=0).astype(BF)
 
     barrier = pltpu.get_barrier_semaphore()
 
-    @pl.loop(1, N)
-    def _(off):
-        _, dev = everyone(off)
-        pl.semaphore_signal(barrier, inc=1, device_id=dev, device_id_type=MESH)
-
-    pl.semaphore_wait(barrier, N - 1)
-
-    @pl.loop(1, N)
-    def _(off):
-        _, dev = everyone(off)
-        remote(place_tx, place_rx.at[me], sem_place.at[0], sem_place.at[1], dev).start()
-
+    for o in ORDER:
+        pl.semaphore_signal(barrier, inc=1, device_id=(g, peer(o)), device_id_type=MESH)
+    for i in range(1, NG):
+        pl.semaphore_signal(barrier, inc=1, device_id=(across(i), d), device_id_type=MESH)
+    pl.semaphore_wait(barrier, ND - 1 + NG - 1)
+
+    for o in ORDER:
+        remote(place_tx, place_rx.at[me], sem_place.at[0], sem_place.at[1], (g, peer(o))).start()
     for o in ORDER:
         remote(meta_tx, meta_rx.at[d], sem_meta.at[0], sem_meta.at[1], (g, peer(o))).start()
     meta_own = pltpu.make_async_copy(meta_tx, meta_rx.at[d], sem_local.at[0])
@@ -110,9 +104,12 @@
     relays = (relay_a, relay_b)
     sends = (send_a, send_b)
     own = []
-    for c, (base, rows) in enumerate(CHUNKS):
-        @pl.loop(0, rows // SUB)
-        def _(s, c=c, base=base, rows=rows):
+
+    def spread_rows(c, lo, hi):
+        base, rows = CHUNKS[c]
+
+        @pl.loop(lo, hi)
+        def _(s):
             for o in ORDER:
                 p = peer(o)
                 remote(
@@ -120,6 +117,9 @@
                     relays[c].at[d, :, pl.ds(pl.multiple_of(s * SUB, SUB), SUB)],
                     sem_p1s.at[c], sem_p1r.at[c], (g, p),
                 ).start()
+
+    spread_rows(0, 0, EARLY)
+    for c, (base, rows) in enumerate(CHUNKS):
         cp = pltpu.make_async_copy(
             q.at[:, pl.ds(pl.multiple_of(base + d * rows, SUB), rows)], relays[c].at[d], sem_local.at[1 + c]
         )
@@ -135,9 +135,9 @@
     q_copy(0).start()
 
     def to_row(a):
-        rep = (lax.rem(iota((TOPK, PAIRS), 1), TOPK) == iota((TOPK, PAIRS), 0)).astype(BF)
+        rep = (iota((ROWS, PAIRS), 1) // TOPK == iota((ROWS, PAIRS), 0)).astype(BF)
         wide = jnp.dot(a[...].astype(F32).astype(BF), rep, preferred_element_type=F32)
-        mine = iota((ROWS, PAIRS), 1) // TOPK == iota((ROWS, PAIRS), 0)
+        mine = lax.rem(iota((TOPK, PAIRS), 1), TOPK) == iota((TOPK, PAIRS), 0)
         return jnp.sum(jnp.where(mine, wide, 0.0), axis=0, keepdims=True)
 
     def to_col(row):
@@ -150,9 +150,15 @@
     def wait_recv_all(ref, sem):
         pltpu.make_async_copy(ref, ref, sem).wait()
 
-    wait_recv_all(place_rx.at[pl.ds(0, N - 1)], sem_place.at[1])
-    sm = pltpu.make_async_copy(place_rx.at[pl.ds(pl.multiple_of(g * ND, ND), ND)], place_sm, sem_local.at[3])
+    group_rows = pl.ds(pl.multiple_of(g * ND, ND), ND)
+    wait_recv_all(place_rx.at[pl.ds(0, ND - 1)], sem_place.at[1])
+    for i in range(1, NG):
+        remote(
+            place_rx.at[group_rows], place_rx.at[group_rows], sem_spread.at[0], sem_spread.at[1], (across(i), d)
+        ).start()
+    sm = pltpu.make_async_copy(place_rx.at[group_rows], place_sm, sem_local.at[3])
     sm.start()
+    wait_recv_all(place_rx.at[pl.ds(0, ND * (NG - 1))], sem_spread.at[1])
 
     hold_of = place_rx[...].reshape(N, 128).astype(F32)
     match = hold_of == expert_row
@@ -184,13 +190,23 @@
 
     unpack_rows(big, tx)
 
-    @pl.loop(1, N)
-    def _(off):
-        t, dev = everyone(off)
-        remote(tx.at[t], rx.at[me], sem_tok.at[0], sem_tok.at[1], dev).start()
-
-    tok_own = pltpu.make_async_copy(tx.at[me], rx.at[me], sem_local.at[4])
+    for i in range(1, NG):
+        t = across(i)
+        remote(
+            tx.at[pl.ds(pl.multiple_of(t * ND, ND), ND)], mid.at[g], sem_tok.at[0], sem_tok.at[1], (t, d)
+        ).start()
+    mid_own = pltpu.make_async_copy(tx.at[group_rows], mid.at[g], sem_local.at[8])
+    mid_own.start()
+    spread_rows(0, EARLY, CHUNKS[0][1] // SUB)
+    mid_own.wait()
+    wait_recv_all(mid.at[pl.ds(0, NG - 1)], sem_tok.at[1])
+    for o in ORDER:
+        p = peer(o)
+        remote(mid.at[:, p], rx.at[d], sem_tok2.at[0], sem_tok2.at[1], (g, p)).start()
+    tok_own = pltpu.make_async_copy(mid.at[:, d], rx.at[d], sem_local.at[4])
     tok_own.start()
+    spread_rows(1, 0, CHUNKS[1][1] // SUB)
+
 
     sm.wait()
 
@@ -218,28 +234,30 @@
     mine_w = place[0]
     got = meta_rx[lax.rem(mine_w // HOLD, ND)]
     slot_m = lax.rem(mine_w, HOLD)
-    keep = (iota((128, 128), 0) == iota((128, 128), 1) + 8 * slot_m).astype(BF)
-    scale_out[...] = jnp.dot(got, keep, preferred_element_type=F32).astype(BF)
+    got_wide = got.astype(F32)
+    mine_scales = jnp.where(slot_m == 0, got_wide[0:8], got_wide[8:16])
+    scale_out[...] = mine_scales[:, 0:KT].astype(BF)
 
     def grow_scales(block, m):
         sel = (iota((128, FF), 0) == iota((128, FF), 1) // TILE + 8 * m).astype(BF)
-        return jnp.dot(block, sel, preferred_element_type=F32).reshape(32, 1, FF)
+        tall = jnp.concatenate([block.astype(F32), jnp.zeros((112, 128), F32)], axis=0).T
+        return jnp.dot(tall[0:32].astype(BF), sel, preferred_element_type=F32).reshape(32, 1, FF)
 
     for m in range(HOLD):
         grow[m] = grow_scales(meta_tx[...], m)
     grow[HOLD] = grow_scales(got, slot_m)
 
     tok_own.wait()
-    wait_recv_all(rx.at[pl.ds(0, N - 1)], sem_tok.at[1])
-
-    pack_rows(rx, big)
+    wait_recv_all(rx.at[pl.ds(0, ND - 1)], sem_tok2.at[1])
+
+    pack_rows(rx, big, True)
 
     code = big[:, D:]
     load_row = jnp.zeros((1, 128), F32)
     for s in range(HOLD + 1):
         count = jnp.sum(jnp.where(code == float(s), 1.0, 0.0), axis=0, keepdims=True)
         load_row = jnp.where(iota((1, 128), 1) == s, count, load_row)
-    load_out[...] = jnp.broadcast_to(load_row, (8, 128)).astype(I32)
+    load_out[...] = load_row[:, 0 : HOLD + 1].astype(I32)
 
     for s in range(HOLD + 1):
         @pl.loop(0, KT)
@@ -303,28 +321,39 @@
 
     unpack_rows(acc, back_tx)
 
-    @pl.loop(1, N)
-    def _(off):
-        t, dev = everyone(off)
-        remote(back_tx.at[t], back_rx.at[me], sem_ret.at[0], sem_ret.at[1], dev).start()
-
-    ret_own = pltpu.make_async_copy(back_tx.at[me], back_rx.at[me], sem_local.at[7])
+    def back_rows(p):
+        return pl.ds(pl.multiple_of(p * NG, NG), NG)
+
+    for o in ORDER:
+        p = peer(o)
+        remote(back_tx.at[back_rows(p)], back_mid.at[:, d], sem_ret.at[0], sem_ret.at[1], (g, p)).start()
+    ret_own = pltpu.make_async_copy(back_tx.at[back_rows(d)], back_mid.at[:, d], sem_local.at[7])
     ret_own.start()
     ret_own.wait()
-    wait_recv_all(back_rx.at[pl.ds(0, N - 1)], sem_ret.at[1])
+    wait_recv_all(back_mid.at[:, pl.ds(0, ND - 1)], sem_ret.at[1])
+    for i in range(1, NG):
+        t = across(i)
+        remote(back_mid.at[t], back_rx.at[group_rows], sem_ret2.at[0], sem_ret2.at[1], (t, d)).start()
+    back_own = pltpu.make_async_copy(back_mid.at[g], back_rx.at[group_rows], sem_local.at[9])
+    back_own.start()
+    back_own.wait()
+    wait_recv_all(back_rx.at[pl.ds(0, ND * (NG - 1))], sem_ret2.at[1])
 
     pack_rows(back_rx, acc)
 
     selected = jnp.dot(placed_t[...], acc[...].astype(BF), preferred_element_type=F32)
     hidden_out[...] = (selected * weight_col[:, 0:1]).astype(BF)
 
-    wait_recv_all(place_rx.at[pl.ds(0, N - 1)], sem_place.at[0])
+    wait_recv_all(place_rx.at[pl.ds(0, ND - 1)], sem_place.at[0])
+    wait_recv_all(place_rx.at[pl.ds(0, ND * (NG - 1))], sem_spread.at[0])
     wait_recv_all(meta_rx.at[pl.ds(0, ND - 1)], sem_meta.at[0])
     for c in range(2):
         wait_recv_all(relays[c].at[pl.ds(0, ND - 1)], sem_p1s.at[c])
         wait_recv_all(sends[c].at[pl.ds(0, ND - 1)], sem_p2s.at[c])
-    wait_recv_all(tx.at[pl.ds(0, N - 1)], sem_tok.at[0])
-    wait_recv_all(back_tx.at[pl.ds(0, N - 1)], sem_ret.at[0])
+    wait_recv_all(mid.at[pl.ds(0, NG - 1)], sem_tok.at[0])
+    wait_recv_all(rx.at[pl.ds(0, ND - 1)], sem_tok2.at[0])
+    wait_recv_all(back_mid.at[:, pl.ds(0, ND - 1)], sem_ret.at[0])
+    wait_recv_all(back_rx.at[pl.ds(0, ND * (NG - 1))], sem_ret2.at[0])
     out_a.wait()
     out_b.wait()
 
@@ -337,8 +366,8 @@
         pltpu.VMEM((1, 128), I32),
         pltpu.VMEM((N, 1, 128), I32),
         pltpu.SMEM((ND, 1, 128), I32),
-        pltpu.VMEM((32, 128), BF),
-        pltpu.VMEM((ND, 32, 128), BF),
+        pltpu.VMEM((16, 128), BF),
+        pltpu.VMEM((ND, 16, 128), BF),
         pltpu.VMEM((ND, HOLD, CHUNKS[0][1], FF), BF),
         pltpu.VMEM((ND, HOLD, CHUNKS[1][1], FF), BF),
         pltpu.VMEM((ND, CHUNKS[0][1], FF), BF),
@@ -346,24 +375,26 @@
         pltpu.VMEM((D, FF), BF),
         pltpu.VMEM((CELLS, WIDE), F32),
         pltpu.VMEM((N, CAP, WIDE), BF),
-        pltpu.VMEM((N, CAP, WIDE), BF),
+        pltpu.VMEM((NG, ND, CAP, WIDE), BF),
+        pltpu.VMEM((ND, NG, CAP, WIDE), BF),
         pltpu.VMEM((HOLD + 1, CELLS, D), BF),
         pltpu.VMEM((CELLS, FF), F32),
         pltpu.VMEM((N, CAP, FF), BF),
+        pltpu.VMEM((NG, ND, CAP, FF), BF),
         pltpu.VMEM((N, CAP, FF), BF),
         pltpu.VMEM((2, QROWS, FF), BF),
         pltpu.VMEM((HOLD + 1, 32, 1, FF), F32),
         pltpu.VMEM((PAIRS, CELLS), BF),
-        dma((2,)), dma((2,)), dma((2,)), dma((2,)), dma((2,)), dma((len(ORDER), 2)),
-        dma((2,)), dma((2,)), dma((8,)), dma((2,)), dma((2,)),
+        dma((2,)), dma((2,)), dma((2,)), dma((2,)), dma((2,)), dma((2,)), dma((len(ORDER), 2)),
+        dma((2,)), dma((2,)), dma((2,)), dma((2,)), dma((10,)), dma((2,)), dma((2,)),
     ]
     new_weights, scale_tile, hidden, load = pl.pallas_call(
         kernel,
         out_shape=(
             jax.ShapeDtypeStruct((D, FF), BF),
-            jax.ShapeDtypeStruct((32, 128), BF),
+            jax.ShapeDtypeStruct((8, KT), BF),
             jax.ShapeDtypeStruct((PAIRS, FF), BF),
-            jax.ShapeDtypeStruct((8, 128), I32),
+            jax.ShapeDtypeStruct((1, HOLD + 1), I32),
         ),
         in_specs=[
             anywhere, vmem, pl.BlockSpec(memory_space=pltpu.SMEM), vmem, vmem, vmem, vmem,
@@ -373,12 +404,15 @@
         compiler_params=pltpu.CompilerParams(
             collective_id=0, has_side_effects=True, vmem_limit_bytes=64000 * 1024
         ),
-    )(primary_q, primary_scales, new_place, tokens, experts, replica, route_num)
+    )(
+        primary_q, primary_scales.transpose(0, 2, 1), new_place, tokens,
+        experts.T, replica.T, route_num.T,
+    )
     return (
         new_weights.reshape(1, D, FF),
-        scale_tile[:KT, :8].reshape(1, KT, 8),
+        scale_tile.T.reshape(1, KT, 8),
         hidden.reshape(ROWS, TOPK, FF),
-        load[0:1, : HOLD + 1],
+        load,
     )
 
 

time: 354 us -> 327 us (0.924)
  Pallas kernels: 337 us -> 313 us
  local copies, waits for them, and re-layouts: 15.7 us -> 8.82 us
    pallas_call x1, Pallas kernels: 337 us -> 313 us  [per_device(): pl.pallas_call(kernel, out_shape=(jax.ShapeDtypeStruct((D, FF), BF), jax....]
    unnamed x9 -> x10, local copies, waits for them, and re-layouts: 13.8 us -> 8.82 us
where the time goes in v2:
time: 327 us; the launch traced here: 324 us
  Pallas kernels  313 us (96%)
  local copies, waits for them, and re-layouts  8.82 us (3%)
    pallas_call x1, Pallas kernels, per_device(): pl.pallas_call(kernel, out_shape=(jax.ShapeDtypeStruct((D, FF), BF), jax....  313 us
    unnamed x10, local copies, waits for them, and re-layouts  8.82 us

profile of v2, /device:TPU:1, one launch (start us, length us, event | category | flops | bytes accessed | tf_op | source)
XLA Modules:
  0.0 323.6 jit_solution(14538609494744069673)
XLA Ops:
  1.3 313.4 %shard_map.102 = (bf16[3584,1024]{1,0:T(8,128)(2,1)}, bf16[8,28]{1,0:T(8,128)(2,1)}, bf16[128,1024]{1,0:T(8,128)(2,1)}, s32[1,3]{1,0:T(1,128)}) custom-call(bf16[2,3584,1024]{2,1,0:T(8,128)(2,1)} %q.1, bf16[2,8,28]{2,1,0:T(8,128)(2,1)} %bitcast.11, s32[1]{0:T(128)S(6)} %copy.15.place, bf16[16,3584]{1,0:T(8,128)(2,1)} %tokens.1, s32[8,16]{1,0:T(8,128)} %bitcast.12, ...), custom_call_target="tpu_custom_call" | custom-call | tf_op jit(solution)/shard_map/pallas_call | solution.py:391
  314.7 0.0 copy-start.1
  314.7 0.0 copy-start
  314.7 0.0 copy-start.2
  314.8 7.0 %copy.16 = bf16[1,3584,1024]{2,1,0:T(8,128)(2,1)} copy(bf16[1,3584,1024]{2,1,0:T(8,128)(2,1)} %bitcast.9) | data formatting | bytes 14680064
  321.8 0.0 copy-done.1
  321.8 0.6 copy.17
  322.4 0.0 copy-done
  322.4 0.7 copy.18
  323.1 0.0 copy-done.2
  323.1 0.5 copy.19
Async XLA Ops:
  314.7 7.0 %copy-start.1 = (bf16[8,28]{1,0:T(8,128)(2,1)S(1)}, bf16[8,28]{1,0:T(8,128)(2,1)}, u32[]{:S(2)}) copy-start(bf16[8,28]{1,0:T(8,128)(2,1)} %get-tuple-element.9) | copy-start | bytes 1348
  314.7 7.6 %copy-start = (bf16[128,1024]{1,0:T(8,128)(2,1)S(1)}, bf16[128,1024]{1,0:T(8,128)(2,1)}, u32[]{:S(2)}) copy-start(bf16[128,1024]{1,0:T(8,128)(2,1)} %get-tuple-element.10) | copy-start | bytes 786436
  314.7 8.3 %copy-start.2 = (s32[1,3]{1,0:T(1,128)S(1)}, s32[1,3]{1,0:T(1,128)}, u32[]{:S(2)}) copy-start(s32[1,3]{1,0:T(1,128)} %get-tuple-element.19) | copy-start | bytes 40

commit v3 on v2

--- a/solution.py
+++ b/solution.py
@@ -28,9 +28,11 @@
     (0, 1), (0, 3), (1, 0), (3, 0), (1, 1), (3, 3), (1, 3), (3, 1),
     (0, 2), (2, 0), (2, 2), (1, 2), (3, 2), (2, 1), (2, 3),
 )
-CHUNKS = ((2048, 96), (0, 128))
-SUB = 16
-EARLY = 3
+CHUNKS = ((0, 0, 0, 512, 0), (0, 1, 512, 384, 1), (1, 0, 0, 512, 1), (1, 1, 512, 384, 0))
+PIECE = 896
+HALF = 512
+SUB = 128
+EARLY = 2
 QROWS = 512
 
 
@@ -58,9 +60,9 @@
     q, scales, place, tokens, experts, replica, route,
     w_out, scale_out, hidden_out, load_out,
     place_tx, place_rx, place_sm, meta_tx, meta_rx,
-    relay_a, relay_b, send_a, send_b, w_new,
+    r0, r1, r2, r3, y0, y1, y2, y3, s0, s1, s2, s3, w_new,
     big, tx, mid, rx, xm, acc, back_tx, back_mid, back_rx, qbuf, grow, placed_t,
-    sem_place, sem_spread, sem_meta, sem_p1s, sem_p1r, sem_p2s, sem_p2r,
+    sem_place, sem_spread, sem_meta, sem_1s, sem_1r, sem_2s, sem_2r, sem_3s, sem_3r, sem_own1, sem_own3,
     sem_tok, sem_tok2, sem_ret, sem_ret2, sem_local, sem_q, sem_w,
 ):
     g = lax.axis_index("group")
@@ -101,30 +103,61 @@
     meta_own = pltpu.make_async_copy(meta_tx, meta_rx.at[d], sem_local.at[0])
     meta_own.start()
 
-    relays = (relay_a, relay_b)
-    sends = (send_a, send_b)
-    own = []
-
-    def spread_rows(c, lo, hi):
-        base, rows = CHUNKS[c]
-
+    relays = (r0, r1, r2, r3)
+    swaps = (y0, y1, y2, y3)
+    sends = (s0, s1, s2, s3)
+
+    def place_of(axis):
+        return (z, x) if axis == 0 else (x, z)
+
+    def dev_of(axis, u, v):
+        return u * 4 + v if axis == 0 else v * 4 + u
+
+    def mod4(i):
+        return lax.rem(i + 8, 4)
+
+    def piece_rows(c, first, n):
+        return pl.ds(pl.multiple_of(c * PIECE + first, 128), n)
+
+    def piece_cols(r, f):
+        return pl.ds(pl.multiple_of(r * 256 + f * 128, 128), 128)
+
+    KINDS = ((0, 0, 0, 1), (0, 1, -1, 0), (1, 0, 1, 0), (-1, 1, -2, 1))
+    FIRST = ((1, 0), (3, 0), (0, 2), (0, 3), (1, 1), (3, 1), (1, 2), (3, 3), (3, 2), (1, 3), (2, 0), (2, 2), (2, 1), (2, 3))
+
+    def supply(k, dv, kind, at, n):
+        f, _, base, rows, axis = CHUNKS[k]
+        u, v = place_of(axis)
+        step, role, piece, line = KINDS[kind]
+        r = mod4(v + dv)
+        src = q.at[:, piece_rows(mod4(u + piece), base + at, n), piece_cols(r, f)]
+        entry = role * 16 + (line * 4 + v) * 2
+        dst = relays[k].at[pl.ds(entry, 2), pl.ds(pl.multiple_of(at, 128), n)]
+        return src, dst, (g, dev_of(axis, mod4(u + step), r))
+
+    def supply_sends(ks, at):
+        for dv, kind in FIRST:
+            for k in ks:
+                src, dst, dev = supply(k, dv, kind, at, SUB)
+                remote(src, dst, sem_1s.at[k], sem_1r.at[k], dev).start()
+
+    def supply_own(k):
+        cps = []
+        for kind in range(2):
+            src, dst, _ = supply(k, 0, kind, 0, CHUNKS[k][3])
+            cps.append(pltpu.make_async_copy(src, dst, sem_own1.at[k, kind]))
+        return cps
+
+    def supply_steps(pair, lo, hi):
         @pl.loop(lo, hi)
-        def _(s):
-            for o in ORDER:
-                p = peer(o)
-                remote(
-                    q.at[:, pl.ds(pl.multiple_of(base + p * rows + s * SUB, SUB), SUB)],
-                    relays[c].at[d, :, pl.ds(pl.multiple_of(s * SUB, SUB), SUB)],
-                    sem_p1s.at[c], sem_p1r.at[c], (g, p),
-                ).start()
-
-    spread_rows(0, 0, EARLY)
-    for c, (base, rows) in enumerate(CHUNKS):
-        cp = pltpu.make_async_copy(
-            q.at[:, pl.ds(pl.multiple_of(base + d * rows, SUB), rows)], relays[c].at[d], sem_local.at[1 + c]
-        )
-        cp.start()
-        own.append(cp)
+        def _(i):
+            supply_sends(pair, i * SUB)
+
+    supply_steps((0, 1), 0, EARLY)
+    own = [supply_own(k) for k in range(4)]
+    for cps in own:
+        for cp in cps:
+            cp.start()
 
     def q_copy(i):
         return pltpu.make_async_copy(
@@ -197,7 +230,8 @@
         ).start()
     mid_own = pltpu.make_async_copy(tx.at[group_rows], mid.at[g], sem_local.at[8])
     mid_own.start()
-    spread_rows(0, EARLY, CHUNKS[0][1] // SUB)
+    supply_steps((0, 1), EARLY, 3)
+    supply_sends((0,), 3 * SUB)
     mid_own.wait()
     wait_recv_all(mid.at[pl.ds(0, NG - 1)], sem_tok.at[1])
     for o in ORDER:
@@ -205,29 +239,89 @@
         remote(mid.at[:, p], rx.at[d], sem_tok2.at[0], sem_tok2.at[1], (g, p)).start()
     tok_own = pltpu.make_async_copy(mid.at[:, d], rx.at[d], sem_local.at[4])
     tok_own.start()
-    spread_rows(1, 0, CHUNKS[1][1] // SUB)
-
+    supply_steps((2, 3), 0, 3)
+    supply_sends((2,), 3 * SUB)
+
+
+    def wanted(axis, u, v):
+        w = place_sm[dev_of(axis, u, v), 0, 0]
+        s = lax.rem(w // HOLD, ND)
+        su, sv = (s // 4, lax.rem(s, 4)) if axis == 0 else (lax.rem(s, 4), s // 4)
+        return su, sv, lax.rem(w, HOLD)
+
+    def entry_of(role, u, want):
+        su, sv, m = want
+        line = (su == u).astype(I32) if role == 0 else (su != u).astype(I32)
+        return role * 16 + (line * 4 + sv) * 2 + m
+
+    def trade(k):
+        _, _, _, rows, axis = CHUNKS[k]
+        u, v = place_of(axis)
+        for cp in own[k]:
+            cp.wait()
+        wait_recv_all(relays[k].at[pl.ds(0, 28)], sem_1r.at[k])
+        for role in range(2):
+            @pl.loop(0, 8)
+            def _(j, role=role):
+                line = mod4(u + (1 if role == 0 else -2) + j // 4)
+                want = wanted(axis, line, lax.rem(j, 4))
+                sends[k][role * 8 + j] = relays[k][entry_of(role, u, want)]
+
+        @pl.loop(0, 8)
+        def _(j):
+            for role in range(2):
+                to = dev_of(axis, mod4(u + (1 if role == 0 else -1)), v)
+                remote(
+                    sends[k].at[role * 8 + j], swaps[k].at[(1 - role) * 8 + j], sem_2s.at[k], sem_2r.at[k], (g, to)
+                ).start()
+
+    def landing(k, role):
+        f, _, base, rows, axis = CHUNKS[k]
+        u, v = place_of(axis)
+        c = u if role == 0 else mod4(u - 1)
+        return w_new.at[f, piece_rows(c, base, rows), pl.ds(pl.multiple_of(v * 128, 128), 128)]
+
+    def own_slot(axis, role):
+        _, v = place_of(axis)
+        return role * 8 + (4 if role == 0 else 0) + v
+
+    def deliver(k):
+        _, _, _, rows, axis = CHUNKS[k]
+        u, v = place_of(axis)
+        wait_recv_all(swaps[k], sem_2r.at[k])
+        wait_recv_all(sends[k], sem_2s.at[k])
+        for role in range(2):
+            @pl.loop(0, 8)
+            def _(j, role=role):
+                line = mod4(u + (-1 if role == 0 else 0) + j // 4)
+                want = wanted(axis, line, lax.rem(j, 4))
+                near = (want[0] == u) | (want[0] == mod4(u + (-1 if role == 0 else 1)))
+                mine = relays[k][entry_of(role, u, want)]
+                other = swaps[k][role * 8 + j]
+                sends[k][role * 8 + j] = jnp.where(near, mine, other)
+        for dv, role, line in (
+            (1, 0, 1), (3, 0, 1), (0, 0, 0), (0, 1, 1), (1, 1, 0), (3, 1, 0), (1, 0, 0), (3, 1, 1),
+            (3, 0, 0), (1, 1, 1), (2, 0, 1), (2, 1, 1), (2, 1, 0), (2, 0, 0),
+        ):
+            r = mod4(v + dv)
+            to = dev_of(axis, mod4(u + line - (1 if role == 0 else 0)), r)
+            remote(
+                sends[k].at[role * 8 + line * 4 + r], landing(k, role), sem_3s.at[k], sem_3r.at[k], (g, to)
+            ).start()
+        for role in range(2):
+            pltpu.make_async_copy(
+                sends[k].at[own_slot(axis, role)], landing(k, role), sem_own3.at[k, role]
+            ).start()
+
+    def delivered(k):
+        for role in range(2):
+            pltpu.make_async_copy(
+                sends[k].at[own_slot(CHUNKS[k][4], role)], landing(k, role), sem_own3.at[k, role]
+            ).wait()
+        got = w_new.at[0, pl.ds(0, 14 * CHUNKS[k][3] // 4), :]
+        pltpu.make_async_copy(got, got, sem_3r.at[k]).wait()
 
     sm.wait()
-
-    def relay_select(c):
-        base, rows = CHUNKS[c]
-        own[c].wait()
-        wait_recv_all(relays[c].at[pl.ds(0, ND - 1)], sem_p1r.at[c])
-
-        @pl.loop(0, ND)
-        def _(p):
-            w = place_sm[p, 0, 0]
-            sends[c][p] = relays[c][lax.rem(w // HOLD, ND), lax.rem(w, HOLD)]
-
-        mine = pl.ds(pl.multiple_of(base + d * rows, SUB), rows)
-        for i, o in enumerate(ORDER):
-            p = peer(o)
-            remote(sends[c].at[p], w_new.at[mine], sem_p2s.at[c], sem_p2r.at[i, c], (g, p)).start()
-        pltpu.make_async_copy(sends[c].at[d], w_new.at[mine], sem_local.at[5 + c]).start()
-
-    relay_select(0)
-    relay_select(1)
 
     meta_own.wait()
     wait_recv_all(meta_rx.at[pl.ds(0, ND - 1)], sem_meta.at[1])
@@ -238,14 +332,16 @@
     mine_scales = jnp.where(slot_m == 0, got_wide[0:8], got_wide[8:16])
     scale_out[...] = mine_scales[:, 0:KT].astype(BF)
 
-    def grow_scales(block, m):
-        sel = (iota((128, FF), 0) == iota((128, FF), 1) // TILE + 8 * m).astype(BF)
+    def grow_scales(block, m, f):
+        tiles = 2 * (iota((128, HALF), 1) // TILE) + f
+        sel = (iota((128, HALF), 0) == tiles + 8 * m).astype(BF)
         tall = jnp.concatenate([block.astype(F32), jnp.zeros((112, 128), F32)], axis=0).T
-        return jnp.dot(tall[0:32].astype(BF), sel, preferred_element_type=F32).reshape(32, 1, FF)
-
-    for m in range(HOLD):
-        grow[m] = grow_scales(meta_tx[...], m)
-    grow[HOLD] = grow_scales(got, slot_m)
+        return jnp.dot(tall[0:32].astype(BF), sel, preferred_element_type=F32).reshape(32, 1, HALF)
+
+    for f in range(2):
+        for m in range(HOLD):
+            grow[m, f] = grow_scales(meta_tx[...], m, f)
+        grow[HOLD, f] = grow_scales(got, slot_m, f)
 
     tok_own.wait()
     wait_recv_all(rx.at[pl.ds(0, ND - 1)], sem_tok2.at[1])
@@ -265,7 +361,7 @@
             cols = pl.ds(pl.multiple_of(k * TILE, TILE), TILE)
             xm[s, :, cols] = jnp.where(code == float(s), big[:, cols], 0.0).astype(BF)
 
-    acc[...] = jnp.zeros((CELLS, FF), F32)
+    acc[...] = jnp.zeros((2, CELLS, HALF), F32)
     n_q = HOLD * (D // QROWS)
 
     @pl.loop(0, n_q)
@@ -276,86 +372,104 @@
         q_copy(i).wait()
         m = i // (D // QROWS)
         tile0 = lax.rem(i, D // QROWS) * (QROWS // TILE)
-        w = qbuf[lax.rem(i, 2)].astype(F32).reshape(QROWS // TILE, TILE, FF)
-        w = (w * grow[m, pl.ds(tile0, QROWS // TILE)]).astype(BF).reshape(QROWS, FF)
         xs = xm[m, :, pl.ds(pl.multiple_of(tile0 * TILE, TILE), QROWS)]
-        acc[...] += jnp.dot(xs, w, preferred_element_type=F32)
-
-    def w_tile(k, n):
-        rows = pl.ds(pl.multiple_of(k * TILE, TILE), n * TILE)
-        w = w_new[rows].astype(F32).reshape(n, TILE, FF)
-        w = (w * grow[HOLD, pl.ds(k, n)]).astype(BF).reshape(n * TILE, FF)
-        acc[...] += jnp.dot(xm[HOLD, :, rows], w, preferred_element_type=F32)
-
-    def w_wait(i, c):
-        base, rows = CHUNKS[c]
-        ref = w_new.at[pl.ds(base, rows)]
-        pltpu.make_async_copy(ref, ref, sem_p2r.at[i, c]).wait()
-
-    def w_own(c):
-        base, rows = CHUNKS[c]
-        mine = pl.ds(pl.multiple_of(base + d * rows, SUB), rows)
-        pltpu.make_async_copy(sends[c].at[d], w_new.at[mine], sem_local.at[5 + c]).wait()
-
-    w_own(0)
-    for i in range(len(ORDER)):
-        w_wait(i, 0)
-    out_a = pltpu.make_async_copy(w_new.at[pl.ds(2048, 1536)], w_out.at[pl.ds(2048, 1536)], sem_w.at[0])
-    out_a.start()
-
-    @pl.loop(0, 3)
-    def _(i):
-        w_tile(16 + 4 * i, 4)
-
-    w_own(1)
-    w_tile(d, 1)
-    for i, o in enumerate(ORDER):
-        w_wait(i, 1)
-        k = lax.rem(z + 4 - o[0], 4) * 4 + lax.rem(x + 4 - o[1], 4)
-        w_tile(k, 1)
-    out_b = pltpu.make_async_copy(w_new.at[pl.ds(0, 2048)], w_out.at[pl.ds(0, 2048)], sem_w.at[1])
-    out_b.start()
-
-    v = acc[...]
-    acc[...] = v / (1.0 + jnp.exp(-v))
-
-    unpack_rows(acc, back_tx)
+        for f in range(2):
+            cols = [qbuf[lax.rem(i, 2), :, 256 * r + 128 * f : 256 * r + 128 * f + 128] for r in range(4)]
+            w = jnp.concatenate(cols, axis=1).astype(F32).reshape(QROWS // TILE, TILE, HALF)
+            w = (w * grow[m, f, pl.ds(tile0, QROWS // TILE)]).astype(BF).reshape(QROWS, HALF)
+            acc[f] += jnp.dot(xs, w, preferred_element_type=F32)
+
+    trade(0)
+    trade(1)
+    deliver(0)
+    trade(2)
+    deliver(1)
+    trade(3)
+    deliver(2)
+    deliver(3)
+
+    def serve(k):
+        f, _, base, rows, _ = CHUNKS[k]
+        delivered(k)
+
+        @pl.loop(0, 4)
+        def _(c):
+            at = piece_rows(c, base, rows)
+            tile0 = c * (PIECE // TILE) + base // TILE
+            w = w_new[f, at, :].astype(F32).reshape(rows // TILE, TILE, HALF)
+            w = (w * grow[HOLD, f, pl.ds(tile0, rows // TILE)]).astype(BF).reshape(rows, HALF)
+            acc[f] += jnp.dot(xm[HOLD, :, at], w, preferred_element_type=F32)
+
+    def write_out(f, r):
+        return pltpu.make_async_copy(
+            w_new.at[f, :, pl.ds(r * 128, 128)], w_out.at[:, pl.ds(r * 256 + f * 128, 128)], sem_w.at[f, r]
+        )
 
     def back_rows(p):
         return pl.ds(pl.multiple_of(p * NG, NG), NG)
 
-    for o in ORDER:
-        p = peer(o)
-        remote(back_tx.at[back_rows(p)], back_mid.at[:, d], sem_ret.at[0], sem_ret.at[1], (g, p)).start()
-    ret_own = pltpu.make_async_copy(back_tx.at[back_rows(d)], back_mid.at[:, d], sem_local.at[7])
-    ret_own.start()
-    ret_own.wait()
-    wait_recv_all(back_mid.at[:, pl.ds(0, ND - 1)], sem_ret.at[1])
-    for i in range(1, NG):
-        t = across(i)
-        remote(back_mid.at[t], back_rx.at[group_rows], sem_ret2.at[0], sem_ret2.at[1], (t, d)).start()
-    back_own = pltpu.make_async_copy(back_mid.at[g], back_rx.at[group_rows], sem_local.at[9])
-    back_own.start()
-    back_own.wait()
-    wait_recv_all(back_rx.at[pl.ds(0, ND * (NG - 1))], sem_ret2.at[1])
-
-    pack_rows(back_rx, acc)
-
-    selected = jnp.dot(placed_t[...], acc[...].astype(BF), preferred_element_type=F32)
-    hidden_out[...] = (selected * weight_col[:, 0:1]).astype(BF)
+    def finish(f):
+        for r in range(4):
+            write_out(f, r).start()
+        v = acc[f]
+        acc[f] = v / (1.0 + jnp.exp(-v))
+        unpack_rows(acc.at[f], back_tx.at[f])
+        for o in ORDER:
+            p = peer(o)
+            remote(
+                back_tx.at[f, back_rows(p)], back_mid.at[f, :, d], sem_ret.at[f, 0], sem_ret.at[f, 1], (g, peer(o))
+            ).start()
+        back_copy(f).start()
+
+    def back_copy(f):
+        return pltpu.make_async_copy(back_tx.at[f, back_rows(d)], back_mid.at[f, :, d], sem_local.at[5 + f])
+
+    def back_own(f):
+        return pltpu.make_async_copy(back_mid.at[f, g], back_rx.at[f, group_rows], sem_local.at[9 + f])
+
+    def back_across(f):
+        back_copy(f).wait()
+        wait_recv_all(back_mid.at[f, :, pl.ds(0, ND - 1)], sem_ret.at[f, 1])
+        for i in range(1, NG):
+            t = across(i)
+            remote(
+                back_mid.at[f, t], back_rx.at[f, group_rows], sem_ret2.at[f, 0], sem_ret2.at[f, 1], (t, d)
+            ).start()
+        back_own(f).start()
+
+    def arrive(f):
+        back_own(f).wait()
+        wait_recv_all(back_rx.at[f, pl.ds(0, ND * (NG - 1))], sem_ret2.at[f, 1])
+        pack_rows(back_rx.at[f], acc.at[f])
+        part = jnp.dot(placed_t[...], acc[f].astype(BF), preferred_element_type=F32)
+        part = (part * weight_col[:, 0:1]).astype(BF)
+        for r in range(4):
+            hidden_out[:, 256 * r + 128 * f : 256 * r + 128 * f + 128] = part[:, 128 * r : 128 * r + 128]
+
+    serve(0)
+    serve(1)
+    finish(0)
+    serve(2)
+    back_across(0)
+    serve(3)
+    finish(1)
+    arrive(0)
+    back_across(1)
+    arrive(1)
 
     wait_recv_all(place_rx.at[pl.ds(0, ND - 1)], sem_place.at[0])
     wait_recv_all(place_rx.at[pl.ds(0, ND * (NG - 1))], sem_spread.at[0])
     wait_recv_all(meta_rx.at[pl.ds(0, ND - 1)], sem_meta.at[0])
-    for c in range(2):
-        wait_recv_all(relays[c].at[pl.ds(0, ND - 1)], sem_p1s.at[c])
-        wait_recv_all(sends[c].at[pl.ds(0, ND - 1)], sem_p2s.at[c])
+    for k in range(4):
+        wait_recv_all(relays[k].at[pl.ds(0, 28)], sem_1s.at[k])
+        wait_recv_all(sends[k].at[pl.ds(0, 14)], sem_3s.at[k])
     wait_recv_all(mid.at[pl.ds(0, NG - 1)], sem_tok.at[0])
     wait_recv_all(rx.at[pl.ds(0, ND - 1)], sem_tok2.at[0])
-    wait_recv_all(back_mid.at[:, pl.ds(0, ND - 1)], sem_ret.at[0])
-    wait_recv_all(back_rx.at[pl.ds(0, ND * (NG - 1))], sem_ret2.at[0])
-    out_a.wait()
-    out_b.wait()
+    for f in range(2):
+        wait_recv_all(back_mid.at[f, :, pl.ds(0, ND - 1)], sem_ret.at[f, 0])
+        wait_recv_all(back_rx.at[f, pl.ds(0, ND * (NG - 1))], sem_ret2.at[f, 0])
+        for r in range(4):
+            write_out(f, r).wait()
 
 
 def per_device(primary_q, primary_scales, new_place, tokens, experts, replica, route_num):
@@ -368,25 +482,25 @@
         pltpu.SMEM((ND, 1, 128), I32),
         pltpu.VMEM((16, 128), BF),
         pltpu.VMEM((ND, 16, 128), BF),
-        pltpu.VMEM((ND, HOLD, CHUNKS[0][1], FF), BF),
-        pltpu.VMEM((ND, HOLD, CHUNKS[1][1], FF), BF),
-        pltpu.VMEM((ND, CHUNKS[0][1], FF), BF),
-        pltpu.VMEM((ND, CHUNKS[1][1], FF), BF),
-        pltpu.VMEM((D, FF), BF),
+        *[pltpu.VMEM((32, c[3], 128), BF) for c in CHUNKS],
+        *[pltpu.VMEM((16, c[3], 128), BF) for c in CHUNKS],
+        *[pltpu.VMEM((16, c[3], 128), BF) for c in CHUNKS],
+        pltpu.VMEM((2, D, HALF), BF),
         pltpu.VMEM((CELLS, WIDE), F32),
         pltpu.VMEM((N, CAP, WIDE), BF),
         pltpu.VMEM((NG, ND, CAP, WIDE), BF),
         pltpu.VMEM((ND, NG, CAP, WIDE), BF),
         pltpu.VMEM((HOLD + 1, CELLS, D), BF),
-        pltpu.VMEM((CELLS, FF), F32),
-        pltpu.VMEM((N, CAP, FF), BF),
-        pltpu.VMEM((NG, ND, CAP, FF), BF),
-        pltpu.VMEM((N, CAP, FF), BF),
+        pltpu.VMEM((2, CELLS, HALF), F32),
+        pltpu.VMEM((2, N, CAP, HALF), BF),
+        pltpu.VMEM((2, NG, ND, CAP, HALF), BF),
+        pltpu.VMEM((2, N, CAP, HALF), BF),
         pltpu.VMEM((2, QROWS, FF), BF),
-        pltpu.VMEM((HOLD + 1, 32, 1, FF), F32),
+        pltpu.VMEM((HOLD + 1, 2, 32, 1, HALF), F32),
         pltpu.VMEM((PAIRS, CELLS), BF),
-        dma((2,)), dma((2,)), dma((2,)), dma((2,)), dma((2,)), dma((2,)), dma((len(ORDER), 2)),
-        dma((2,)), dma((2,)), dma((2,)), dma((2,)), dma((10,)), dma((2,)), dma((2,)),
+        dma((2,)), dma((2,)), dma((2,)), dma((4,)), dma((4,)), dma((4,)), dma((4,)), dma((4,)), dma((4,)),
+        dma((4, 2)), dma((4, 2)),
+        dma((2,)), dma((2,)), dma((2, 2)), dma((2, 2)), dma((11,)), dma((2,)), dma((2, 4)),
     ]
     new_weights, scale_tile, hidden, load = pl.pallas_call(
         kernel,

time: 327 us -> 293 us (0.90)
  Pallas kernels: 313 us -> 282 us
    pallas_call x1, Pallas kernels: 313 us -> 282 us  [per_device(): pl.pallas_call(kernel, out_shape=(jax.ShapeDtypeStruct((D, FF), BF), jax....]
where the time goes in v3:
time: 293 us; the launch traced here: 292 us
  Pallas kernels  282 us (96%)
  local copies, waits for them, and re-layouts  8.82 us (3%)
    pallas_call x1, Pallas kernels, per_device(): pl.pallas_call(kernel, out_shape=(jax.ShapeDtypeStruct((D, FF), BF), jax....  282 us
    unnamed x10, local copies, waits for them, and re-layouts  8.82 us

profile of v3, /device:TPU:1, one launch (start us, length us, event | category | flops | bytes accessed | tf_op | source)
XLA Modules:
  0.0 292.2 jit_solution(10114500010434313469)
XLA Ops:
  1.3 282.1 %shard_map.102 = (bf16[3584,1024]{1,0:T(8,128)(2,1)}, bf16[8,28]{1,0:T(8,128)(2,1)}, bf16[128,1024]{1,0:T(8,128)(2,1)}, s32[1,3]{1,0:T(1,128)}) custom-call(bf16[2,3584,1024]{2,1,0:T(8,128)(2,1)} %q.1, bf16[2,8,28]{2,1,0:T(8,128)(2,1)} %bitcast.11, s32[1]{0:T(128)S(6)} %copy.15.place, bf16[16,3584]{1,0:T(8,128)(2,1)} %tokens.1, s32[8,16]{1,0:T(8,128)} %bitcast.12, ...), custom_call_target="tpu_custom_call" | custom-call | tf_op jit(solution)/shard_map/pallas_call | solution.py:505
  283.4 0.0 copy-start.1
  283.4 0.0 copy-start
  283.4 0.0 copy-start.2
  283.4 7.0 %copy.16 = bf16[1,3584,1024]{2,1,0:T(8,128)(2,1)} copy(bf16[1,3584,1024]{2,1,0:T(8,128)(2,1)} %bitcast.9) | data formatting | bytes 14680064
  290.4 0.0 copy-done.1
  290.4 0.6 copy.17
  291.0 0.0 copy-done
  291.0 0.7 copy.18
  291.7 0.0 copy-done.2
  291.7 0.5 copy.19
Async XLA Ops:
  283.4 7.0 %copy-start.1 = (bf16[8,28]{1,0:T(8,128)(2,1)S(1)}, bf16[8,28]{1,0:T(8,128)(2,1)}, u32[]{:S(2)}) copy-start(bf16[8,28]{1,0:T(8,128)(2,1)} %get-tuple-element.9) | copy-start | bytes 1348
  283.4 7.6 %copy-start = (bf16[128,1024]{1,0:T(8,128)(2,1)S(1)}, bf16[128,1024]{1,0:T(8,128)(2,1)}, u32[]{:S(2)}) copy-start(bf16[128,1024]{1,0:T(8,128)(2,1)} %get-tuple-element.10) | copy-start | bytes 786436
  283.4 8.3 %copy-start.2 = (s32[1,3]{1,0:T(1,128)S(1)}, s32[1,3]{1,0:T(1,128)}, u32[]{:S(2)}) copy-start(s32[1,3]{1,0:T(1,128)} %get-tuple-element.19) | copy-start | bytes 40

commit v4 on v3

--- a/solution.py
+++ b/solution.py
@@ -31,8 +31,8 @@
 CHUNKS = ((0, 0, 0, 512, 0), (0, 1, 512, 384, 1), (1, 0, 0, 512, 1), (1, 1, 512, 384, 0))
 PIECE = 896
 HALF = 512
-SUB = 128
-EARLY = 2
+SUB = 64
+EARLY = 4
 QROWS = 512
 
 
@@ -58,12 +58,12 @@
 
 def kernel(
     q, scales, place, tokens, experts, replica, route,
-    w_out, scale_out, hidden_out, load_out,
+    w_new, scale_out, hidden_out, load_out,
     place_tx, place_rx, place_sm, meta_tx, meta_rx,
-    r0, r1, r2, r3, y0, y1, y2, y3, s0, s1, s2, s3, w_new,
+    r0, r1, r2, r3, y0, y1, y2, y3, s0, s1, s2, s3,
     big, tx, mid, rx, xm, acc, back_tx, back_mid, back_rx, qbuf, grow, placed_t,
     sem_place, sem_spread, sem_meta, sem_1s, sem_1r, sem_2s, sem_2r, sem_3s, sem_3r, sem_own1, sem_own3,
-    sem_tok, sem_tok2, sem_ret, sem_ret2, sem_local, sem_q, sem_w,
+    sem_tok, sem_tok2, sem_ret, sem_ret2, sem_local, sem_q,
 ):
     g = lax.axis_index("group")
     d = lax.axis_index("dev")
@@ -117,7 +117,7 @@
         return lax.rem(i + 8, 4)
 
     def piece_rows(c, first, n):
-        return pl.ds(pl.multiple_of(c * PIECE + first, 128), n)
+        return pl.ds(pl.multiple_of(c * PIECE + first, SUB), n)
 
     def piece_cols(r, f):
         return pl.ds(pl.multiple_of(r * 256 + f * 128, 128), 128)
@@ -132,7 +132,7 @@
         r = mod4(v + dv)
         src = q.at[:, piece_rows(mod4(u + piece), base + at, n), piece_cols(r, f)]
         entry = role * 16 + (line * 4 + v) * 2
-        dst = relays[k].at[pl.ds(entry, 2), pl.ds(pl.multiple_of(at, 128), n)]
+        dst = relays[k].at[pl.ds(entry, 2), pl.ds(pl.multiple_of(at, SUB), n)]
         return src, dst, (g, dev_of(axis, mod4(u + step), r))
 
     def supply_sends(ks, at):
@@ -230,8 +230,8 @@
         ).start()
     mid_own = pltpu.make_async_copy(tx.at[group_rows], mid.at[g], sem_local.at[8])
     mid_own.start()
-    supply_steps((0, 1), EARLY, 3)
-    supply_sends((0,), 3 * SUB)
+    supply_steps((0, 1), EARLY, 6)
+    supply_steps((0,), 6, 8)
     mid_own.wait()
     wait_recv_all(mid.at[pl.ds(0, NG - 1)], sem_tok.at[1])
     for o in ORDER:
@@ -239,8 +239,8 @@
         remote(mid.at[:, p], rx.at[d], sem_tok2.at[0], sem_tok2.at[1], (g, p)).start()
     tok_own = pltpu.make_async_copy(mid.at[:, d], rx.at[d], sem_local.at[4])
     tok_own.start()
-    supply_steps((2, 3), 0, 3)
-    supply_sends((2,), 3 * SUB)
+    supply_steps((2, 3), 0, 6)
+    supply_steps((2,), 6, 8)
 
 
     def wanted(axis, u, v):
@@ -254,7 +254,7 @@
         line = (su == u).astype(I32) if role == 0 else (su != u).astype(I32)
         return role * 16 + (line * 4 + sv) * 2 + m
 
-    def trade(k):
+    def trade_pick(k):
         _, _, _, rows, axis = CHUNKS[k]
         u, v = place_of(axis)
         for cp in own[k]:
@@ -267,25 +267,38 @@
                 want = wanted(axis, line, lax.rem(j, 4))
                 sends[k][role * 8 + j] = relays[k][entry_of(role, u, want)]
 
+    def trade(pair):
+        for k in pair:
+            trade_pick(k)
+
         @pl.loop(0, 8)
         def _(j):
             for role in range(2):
-                to = dev_of(axis, mod4(u + (1 if role == 0 else -1)), v)
-                remote(
-                    sends[k].at[role * 8 + j], swaps[k].at[(1 - role) * 8 + j], sem_2s.at[k], sem_2r.at[k], (g, to)
-                ).start()
+                for k in pair:
+                    axis = CHUNKS[k][4]
+                    u, v = place_of(axis)
+                    to = dev_of(axis, mod4(u + (1 if role == 0 else -1)), v)
+                    remote(
+                        sends[k].at[role * 8 + j], swaps[k].at[(1 - role) * 8 + j],
+                        sem_2s.at[k], sem_2r.at[k], (g, to),
+                    ).start()
 
     def landing(k, role):
         f, _, base, rows, axis = CHUNKS[k]
         u, v = place_of(axis)
         c = u if role == 0 else mod4(u - 1)
-        return w_new.at[f, piece_rows(c, base, rows), pl.ds(pl.multiple_of(v * 128, 128), 128)]
+        return w_new.at[piece_rows(c, base, rows), piece_cols(v, f)]
+
+    LAST = (
+        (1, 0, 1), (3, 0, 1), (0, 0, 0), (0, 1, 1), (1, 1, 0), (3, 1, 0), (1, 0, 0), (3, 1, 1),
+        (3, 0, 0), (1, 1, 1), (2, 0, 1), (2, 1, 1), (2, 1, 0), (2, 0, 0),
+    )
 
     def own_slot(axis, role):
         _, v = place_of(axis)
         return role * 8 + (4 if role == 0 else 0) + v
 
-    def deliver(k):
+    def deliver_pick(k):
         _, _, _, rows, axis = CHUNKS[k]
         u, v = place_of(axis)
         wait_recv_all(swaps[k], sem_2r.at[k])
@@ -299,26 +312,30 @@
                 mine = relays[k][entry_of(role, u, want)]
                 other = swaps[k][role * 8 + j]
                 sends[k][role * 8 + j] = jnp.where(near, mine, other)
-        for dv, role, line in (
-            (1, 0, 1), (3, 0, 1), (0, 0, 0), (0, 1, 1), (1, 1, 0), (3, 1, 0), (1, 0, 0), (3, 1, 1),
-            (3, 0, 0), (1, 1, 1), (2, 0, 1), (2, 1, 1), (2, 1, 0), (2, 0, 0),
-        ):
-            r = mod4(v + dv)
-            to = dev_of(axis, mod4(u + line - (1 if role == 0 else 0)), r)
-            remote(
-                sends[k].at[role * 8 + line * 4 + r], landing(k, role), sem_3s.at[k], sem_3r.at[k], (g, to)
-            ).start()
         for role in range(2):
             pltpu.make_async_copy(
                 sends[k].at[own_slot(axis, role)], landing(k, role), sem_own3.at[k, role]
             ).start()
+
+    def deliver(pair):
+        for k in pair:
+            deliver_pick(k)
+        for dv, role, line in LAST:
+            for k in pair:
+                axis = CHUNKS[k][4]
+                u, v = place_of(axis)
+                r = mod4(v + dv)
+                to = dev_of(axis, mod4(u + line - (1 if role == 0 else 0)), r)
+                remote(
+                    sends[k].at[role * 8 + line * 4 + r], landing(k, role), sem_3s.at[k], sem_3r.at[k], (g, to)
+                ).start()
 
     def delivered(k):
         for role in range(2):
             pltpu.make_async_copy(
                 sends[k].at[own_slot(CHUNKS[k][4], role)], landing(k, role), sem_own3.at[k, role]
             ).wait()
-        got = w_new.at[0, pl.ds(0, 14 * CHUNKS[k][3] // 4), :]
+        got = w_new.at[pl.ds(0, 14 * CHUNKS[k][3] // 8), :]
         pltpu.make_async_copy(got, got, sem_3r.at[k]).wait()
 
     sm.wait()
@@ -379,14 +396,10 @@
             w = (w * grow[m, f, pl.ds(tile0, QROWS // TILE)]).astype(BF).reshape(QROWS, HALF)
             acc[f] += jnp.dot(xs, w, preferred_element_type=F32)
 
-    trade(0)
-    trade(1)
-    deliver(0)
-    trade(2)
-    deliver(1)
-    trade(3)
-    deliver(2)
-    deliver(3)
+    trade((0, 1))
+    trade((2, 3))
+    deliver((0, 1))
+    deliver((2, 3))
 
     def serve(k):
         f, _, base, rows, _ = CHUNKS[k]
@@ -396,21 +409,15 @@
         def _(c):
             at = piece_rows(c, base, rows)
             tile0 = c * (PIECE // TILE) + base // TILE
-            w = w_new[f, at, :].astype(F32).reshape(rows // TILE, TILE, HALF)
+            cols = [w_new[at, 256 * r + 128 * f : 256 * r + 128 * f + 128] for r in range(4)]
+            w = jnp.concatenate(cols, axis=1).astype(F32).reshape(rows // TILE, TILE, HALF)
             w = (w * grow[HOLD, f, pl.ds(tile0, rows // TILE)]).astype(BF).reshape(rows, HALF)
             acc[f] += jnp.dot(xm[HOLD, :, at], w, preferred_element_type=F32)
 
-    def write_out(f, r):
-        return pltpu.make_async_copy(
-            w_new.at[f, :, pl.ds(r * 128, 128)], w_out.at[:, pl.ds(r * 256 + f * 128, 128)], sem_w.at[f, r]
-        )
-
     def back_rows(p):
         return pl.ds(pl.multiple_of(p * NG, NG), NG)
 
     def finish(f):
-        for r in range(4):
-            write_out(f, r).start()
         v = acc[f]
         acc[f] = v / (1.0 + jnp.exp(-v))
         unpack_rows(acc.at[f], back_tx.at[f])
@@ -468,8 +475,6 @@
     for f in range(2):
         wait_recv_all(back_mid.at[f, :, pl.ds(0, ND - 1)], sem_ret.at[f, 0])
         wait_recv_all(back_rx.at[f, pl.ds(0, ND * (NG - 1))], sem_ret2.at[f, 0])
-        for r in range(4):
-            write_out(f, r).wait()
 
 
 def per_device(primary_q, primary_scales, new_place, tokens, experts, replica, route_num):
@@ -485,7 +490,6 @@
         *[pltpu.VMEM((32, c[3], 128), BF) for c in CHUNKS],
         *[pltpu.VMEM((16, c[3], 128), BF) for c in CHUNKS],
         *[pltpu.VMEM((16, c[3], 128), BF) for c in CHUNKS],
-        pltpu.VMEM((2, D, HALF), BF),
         pltpu.VMEM((CELLS, WIDE), F32),
         pltpu.VMEM((N, CAP, WIDE), BF),
         pltpu.VMEM((NG, ND, CAP, WIDE), BF),
@@ -500,23 +504,23 @@
         pltpu.VMEM((PAIRS, CELLS), BF),
         dma((2,)), dma((2,)), dma((2,)), dma((4,)), dma((4,)), dma((4,)), dma((4,)), dma((4,)), dma((4,)),
         dma((4, 2)), dma((4, 2)),
-        dma((2,)), dma((2,)), dma((2, 2)), dma((2, 2)), dma((11,)), dma((2,)), dma((2, 4)),
+        dma((2,)), dma((2,)), dma((2, 2)), dma((2, 2)), dma((11,)), dma((2,)),
     ]
     new_weights, scale_tile, hidden, load = pl.pallas_call(
         kernel,
         out_shape=(
-            jax.ShapeDtypeStruct((D, FF), BF),
-            jax.ShapeDtypeStruct((8, KT), BF),
-            jax.ShapeDtypeStruct((PAIRS, FF), BF),
-            jax.ShapeDtypeStruct((1, HOLD + 1), I32),
+            pltpu.VMEM((D, FF), BF),
+            pltpu.VMEM((8, KT), BF),
+            pltpu.VMEM((PAIRS, FF), BF),
+            pltpu.VMEM((1, HOLD + 1), I32),
         ),
         in_specs=[
             anywhere, vmem, pl.BlockSpec(memory_space=pltpu.SMEM), vmem, vmem, vmem, vmem,
         ],
-        out_specs=(anywhere, vmem, vmem, vmem),
+        out_specs=(vmem, vmem, vmem, vmem),
         scratch_shapes=scratch,
         compiler_params=pltpu.CompilerParams(
-            collective_id=0, has_side_effects=True, vmem_limit_bytes=64000 * 1024
+            collective_id=0, has_side_effects=True, vmem_limit_bytes=56000 * 1024
         ),
     )(
         primary_q, primary_scales.transpose(0, 2, 1), new_place, tokens,

time: 293 us -> 283 us (0.966)
  Pallas kernels: 282 us -> 276 us
  local copies, waits for them, and re-layouts: 8.82 us -> 4.84 us
    pallas_call x1, Pallas kernels: 282 us -> 276 us  [per_device(): pl.pallas_call(kernel, out_shape=(pltpu.VMEM((D, FF), BF), pltpu.VMEM((8,...]
    unnamed x10 -> x4, local copies, waits for them, and re-layouts: 8.82 us -> 4.84 us
where the time goes in v4:
time: 283 us; the launch traced here: 282 us
  Pallas kernels  276 us (98%)
  local copies, waits for them, and re-layouts  4.84 us (2%)
    pallas_call x1, Pallas kernels, per_device(): pl.pallas_call(kernel, out_shape=(pltpu.VMEM((D, FF), BF), pltpu.VMEM((8,...  276 us

profile of v4, /device:TPU:1, one launch (start us, length us, event | category | flops | bytes accessed | tf_op | source)
XLA Modules:
  0.0 282.1 jit_solution(11094376225122793113)
XLA Ops:
  1.3 276.0 %shard_map.102 = (bf16[3584,1024]{1,0:T(8,128)(2,1)S(1)}, bf16[8,28]{1,0:T(8,128)(2,1)S(1)}, bf16[128,1024]{1,0:T(8,128)(2,1)S(1)}, s32[1,3]{1,0:T(1,128)S(1)}) custom-call(bf16[2,3584,1024]{2,1,0:T(8,128)(2,1)} %q.1, bf16[2,8,28]{2,1,0:T(8,128)(2,1)} %bitcast.12, s32[1]{0:T(128)S(6)} %copy.19.place, bf16[16,3584]{1,0:T(8,128)(2,1)} %tokens.1, ...), custom_call_target="tpu_custom_call" | custom-call | tf_op jit(solution)/shard_map/pallas_call | solution.py:509
  277.3 3.1 %copy.15 = bf16[1,3584,1024]{2,1,0:T(8,128)(2,1)} copy(bf16[1,3584,1024]{2,1,0:T(8,128)(2,1)S(1)} %bitcast.9) | data formatting | bytes 14680064
  280.3 0.6 copy.16
  280.9 0.5 copy.18
  281.4 0.7 copy.17

commit v5 on v4

--- a/solution.py
+++ b/solution.py
@@ -82,18 +82,19 @@
     def across(i):
         return lax.rem(g + i, NG)
 
+    barrier = pltpu.get_barrier_semaphore()
+
+    for o in ORDER:
+        pl.semaphore_signal(barrier, inc=1, device_id=(g, peer(o)), device_id_type=MESH)
+    for i in range(1, NG):
+        pl.semaphore_signal(barrier, inc=1, device_id=(across(i), d), device_id_type=MESH)
+
     place_tx[...] = jnp.full((1, 128), place[0], I32)
     place_rx[me] = jnp.full((1, 128), place[0], I32)
     widen = (iota((KT, 128), 0) == iota((KT, 128), 1)).astype(BF)
     spread = [jnp.dot(scales[m], widen, preferred_element_type=F32) for m in range(HOLD)]
     meta_tx[...] = jnp.concatenate(spread, axis=0).astype(BF)
 
-    barrier = pltpu.get_barrier_semaphore()
-
-    for o in ORDER:
-        pl.semaphore_signal(barrier, inc=1, device_id=(g, peer(o)), device_id_type=MESH)
-    for i in range(1, NG):
-        pl.semaphore_signal(barrier, inc=1, device_id=(across(i), d), device_id_type=MESH)
     pl.semaphore_wait(barrier, ND - 1 + NG - 1)
 
     for o in ORDER:
@@ -313,30 +314,25 @@
                 other = swaps[k][role * 8 + j]
                 sends[k][role * 8 + j] = jnp.where(near, mine, other)
         for role in range(2):
-            pltpu.make_async_copy(
-                sends[k].at[own_slot(axis, role)], landing(k, role), sem_own3.at[k, role]
-            ).start()
+            own_part(k, role).start()
 
     def deliver(pair):
         for k in pair:
             deliver_pick(k)
-        for dv, role, line in LAST:
+        for i, (dv, role, line) in enumerate(LAST):
             for k in pair:
                 axis = CHUNKS[k][4]
                 u, v = place_of(axis)
                 r = mod4(v + dv)
                 to = dev_of(axis, mod4(u + line - (1 if role == 0 else 0)), r)
                 remote(
-                    sends[k].at[role * 8 + line * 4 + r], landing(k, role), sem_3s.at[k], sem_3r.at[k], (g, to)
+                    sends[k].at[role * 8 + line * 4 + r], landing(k, role), sem_3s.at[k], sem_3r.at[k, i], (g, to)
                 ).start()
 
-    def delivered(k):
-        for role in range(2):
-            pltpu.make_async_copy(
-                sends[k].at[own_slot(CHUNKS[k][4], role)], landing(k, role), sem_own3.at[k, role]
-            ).wait()
-        got = w_new.at[pl.ds(0, 14 * CHUNKS[k][3] // 8), :]
-        pltpu.make_async_copy(got, got, sem_3r.at[k]).wait()
+    def own_part(k, role):
+        return pltpu.make_async_copy(
+            sends[k].at[own_slot(CHUNKS[k][4], role)], landing(k, role), sem_own3.at[k, role]
+        )
 
     sm.wait()
 
@@ -401,18 +397,30 @@
     deliver((0, 1))
     deliver((2, 3))
 
-    def serve(k):
+    def serve_part(k, c, r):
         f, _, base, rows, _ = CHUNKS[k]
-        delivered(k)
-
-        @pl.loop(0, 4)
-        def _(c):
-            at = piece_rows(c, base, rows)
-            tile0 = c * (PIECE // TILE) + base // TILE
-            cols = [w_new[at, 256 * r + 128 * f : 256 * r + 128 * f + 128] for r in range(4)]
-            w = jnp.concatenate(cols, axis=1).astype(F32).reshape(rows // TILE, TILE, HALF)
-            w = (w * grow[HOLD, f, pl.ds(tile0, rows // TILE)]).astype(BF).reshape(rows, HALF)
-            acc[f] += jnp.dot(xm[HOLD, :, at], w, preferred_element_type=F32)
+        at = piece_rows(c, base, rows)
+        tiles = pl.ds(c * (PIECE // TILE) + base // TILE, rows // TILE)
+        cols = pl.ds(pl.multiple_of(r * 128, 128), 128)
+        w = w_new[at, piece_cols(r, f)].astype(F32).reshape(rows // TILE, TILE, 128)
+        w = (w * grow[HOLD, f, tiles, :, cols]).astype(BF).reshape(rows, 128)
+        acc[f, :, cols] += jnp.dot(xm[HOLD, :, at], w, preferred_element_type=F32)
+
+    def serve_own(pair):
+        for k in pair:
+            u, v = place_of(CHUNKS[k][4])
+            for role in range(2):
+                own_part(k, role).wait()
+                serve_part(k, u if role == 0 else mod4(u - 1), v)
+
+    def serve(pair, lo, hi):
+        for i, (dv, role, line) in list(enumerate(LAST))[lo:hi]:
+            for k in pair:
+                u, v = place_of(CHUNKS[k][4])
+                got = w_new.at[pl.ds(0, CHUNKS[k][3]), pl.ds(0, 128)]
+                pltpu.make_async_copy(got, got, sem_3r.at[k, i]).wait()
+                c = mod4(u - line + (1 if role == 0 else -1))
+                serve_part(k, c, mod4(v - dv))
 
     def back_rows(p):
         return pl.ds(pl.multiple_of(p * NG, NG), NG)
@@ -453,13 +461,13 @@
         for r in range(4):
             hidden_out[:, 256 * r + 128 * f : 256 * r + 128 * f + 128] = part[:, 128 * r : 128 * r + 128]
 
-    serve(0)
-    serve(1)
+    serve_own((0, 1))
+    serve((0, 1), 0, 14)
     finish(0)
-    serve(2)
+    serve_own((2, 3))
+    serve((2, 3), 0, 14)
+    finish(1)
     back_across(0)
-    serve(3)
-    finish(1)
     arrive(0)
     back_across(1)
     arrive(1)
@@ -475,6 +483,20 @@
     for f in range(2):
         wait_recv_all(back_mid.at[f, :, pl.ds(0, ND - 1)], sem_ret.at[f, 0])
         wait_recv_all(back_rx.at[f, pl.ds(0, ND * (NG - 1))], sem_ret2.at[f, 0])
+
+
+def store(w, scale, hidden, load, w_out, scale_out, hidden_out, load_out, sems):
+    n = 4
+    part = D // n
+    copies = [
+        pltpu.make_async_copy(w.at[pl.ds(i * part, part)], w_out.at[pl.ds(i * part, part)], sems.at[i]) for i in range(n)
+    ]
+    for i, (a, b) in enumerate(((scale, scale_out), (hidden, hidden_out), (load, load_out))):
+        copies.append(pltpu.make_async_copy(a, b, sems.at[n + i]))
+    for c in copies:
+        c.start()
+    for c in copies:
+        c.wait()
 
 
 def per_device(primary_q, primary_scales, new_place, tokens, experts, replica, route_num):
@@ -502,7 +524,7 @@
         pltpu.VMEM((2, QROWS, FF), BF),
         pltpu.VMEM((HOLD + 1, 2, 32, 1, HALF), F32),
         pltpu.VMEM((PAIRS, CELLS), BF),
-        dma((2,)), dma((2,)), dma((2,)), dma((4,)), dma((4,)), dma((4,)), dma((4,)), dma((4,)), dma((4,)),
+        dma((2,)), dma((2,)), dma((2,)), dma((4,)), dma((4,)), dma((4,)), dma((4,)), dma((4,)), dma((4, 14)),
         dma((4, 2)), dma((4, 2)),
         dma((2,)), dma((2,)), dma((2, 2)), dma((2, 2)), dma((11,)), dma((2,)),
     ]
@@ -526,6 +548,22 @@
         primary_q, primary_scales.transpose(0, 2, 1), new_place, tokens,
         experts.T, replica.T, route_num.T,
     )
+    results = [
+        pltpu.with_memory_space_constraint(a, pltpu.VMEM) for a in (new_weights, scale_tile, hidden, load)
+    ]
+    new_weights, scale_tile, hidden, load = pl.pallas_call(
+        store,
+        out_shape=(
+            jax.ShapeDtypeStruct((D, FF), BF),
+            jax.ShapeDtypeStruct((8, KT), BF),
+            jax.ShapeDtypeStruct((PAIRS, FF), BF),
+            jax.ShapeDtypeStruct((1, HOLD + 1), I32),
+        ),
+        in_specs=[vmem] * 4,
+        out_specs=(anywhere,) * 4,
+        scratch_shapes=[dma((7,))],
+        compiler_params=pltpu.CompilerParams(vmem_limit_bytes=1024 * 1024),
+    )(*results)
     return (
         new_weights.reshape(1, D, FF),
         scale_tile.T.reshape(1, KT, 8),

time: 283 us -> 280 us (0.989)
  local copies, waits for them, and re-layouts: 4.84 us -> 0 us
    unnamed x4 -> x0, local copies, waits for them, and re-layouts: 4.84 us -> none
    pallas_call x0 -> x1, Pallas kernels: none -> 3.14 us  [per_device(): pl.pallas_call(store, out_shape=(jax.ShapeDtypeStruct((D, FF), BF), jax.S...]
where the time goes in v5:
time: 280 us
  Pallas kernels  278 us (99%)
    pallas_call x1, Pallas kernels, per_device(): pl.pallas_call(kernel, out_shape=(pltpu.VMEM((D, FF), BF), pltpu.VMEM((8,...  275 us

profile of v5, /device:TPU:1, one launch (start us, length us, event | category | flops | bytes accessed | tf_op | source)
XLA Modules:
  0.0 279.7 jit_solution(14074747455419272679)
XLA Ops:
  1.3 275.2 %shard_map.102 = (bf16[3584,1024]{1,0:T(8,128)(2,1)S(1)}, bf16[8,28]{1,0:T(8,128)(2,1)S(1)}, bf16[128,1024]{1,0:T(8,128)(2,1)S(1)}, s32[1,3]{1,0:T(1,128)S(1)}) custom-call(bf16[2,3584,1024]{2,1,0:T(8,128)(2,1)} %q.1, bf16[2,8,28]{2,1,0:T(8,128)(2,1)} %bitcast.9, s32[1]{0:T(128)S(6)} %copy.11.place, bf16[16,3584]{1,0:T(8,128)(2,1)} %tokens.1, ...), custom_call_target="tpu_custom_call" | custom-call | tf_op jit(solution)/shard_map/pallas_call | solution.py:531
  276.4 3.1 %shard_map.103 = (bf16[3584,1024]{1,0:T(8,128)(2,1)}, bf16[8,28]{1,0:T(8,128)(2,1)}, bf16[128,1024]{1,0:T(8,128)(2,1)}, s32[1,3]{1,0:T(1,128)}) custom-call(bf16[3584,1024]{1,0:T(8,128)(2,1)S(1)} %get-tuple-element.12.w, bf16[8,28]{1,0:T(8,128)(2,1)S(1)} %get-tuple-element.13.scale, bf16[128,1024]{1,0:T(8,128)(2,1)S(1)} %get-tuple-element.14.hidden, ...), custom_call_target="tpu_custom_call" | custom-call | tf_op jit(solution)/shard_map/pallas_call | solution.py:554

commit v6 on v5

--- a/solution.py
+++ b/solution.py
@@ -46,6 +46,13 @@
         v = flat[pl.ds(pl.multiple_of(8 * i, 8), 8), :]
         for j in range(4):
             blocks[4 * i + j] = v[2 * j : 2 * j + 2].astype(BF)
+
+
+def unpack_part(flat, blocks, p):
+    for h in range(2):
+        v = flat[pl.ds(pl.multiple_of(16 * p + 8 * h, 8), 8), :]
+        for j in range(4):
+            blocks[8 * p + 4 * h + j] = v[2 * j : 2 * j + 2].astype(BF)
 
 
 def pack_rows(blocks, flat, nested=False):
@@ -428,13 +435,17 @@
     def finish(f):
         v = acc[f]
         acc[f] = v / (1.0 + jnp.exp(-v))
-        unpack_rows(acc.at[f], back_tx.at[f])
-        for o in ORDER:
-            p = peer(o)
-            remote(
-                back_tx.at[f, back_rows(p)], back_mid.at[f, :, d], sem_ret.at[f, 0], sem_ret.at[f, 1], (g, peer(o))
-            ).start()
+        peers = [peer(o) for o in ORDER] + [d]
+        for i, p in enumerate(peers):
+            unpack_part(acc.at[f], back_tx.at[f], p)
+            if i > 0:
+                back_send(f, peers[i - 1])
         back_copy(f).start()
+
+    def back_send(f, p):
+        remote(
+            back_tx.at[f, back_rows(p)], back_mid.at[f, :, d], sem_ret.at[f, 0], sem_ret.at[f, 1], (g, p)
+        ).start()
 
     def back_copy(f):
         return pltpu.make_async_copy(back_tx.at[f, back_rows(d)], back_mid.at[f, :, d], sem_local.at[5 + f])
@@ -468,8 +479,8 @@
     serve((2, 3), 0, 14)
     finish(1)
     back_across(0)
+    back_across(1)
     arrive(0)
-    back_across(1)
     arrive(1)
 
     wait_recv_all(place_rx.at[pl.ds(0, ND - 1)], sem_place.at[0])

time: 280 us -> 277 us (0.989)
  Pallas kernels: 278 us -> 275 us
    pallas_call x1, Pallas kernels: 275 us -> 272 us  [per_device(): pl.pallas_call(kernel, out_shape=(pltpu.VMEM((D, FF), BF), pltpu.VMEM((8,...]
where the time goes in v6:
time: 277 us
  Pallas kernels  275 us (99%)
    pallas_call x1, Pallas kernels, per_device(): pl.pallas_call(kernel, out_shape=(pltpu.VMEM((D, FF), BF), pltpu.VMEM((8,...  272 us

profile of v6, /device:TPU:1, one launch (start us, length us, event | category | flops | bytes accessed | tf_op | source)
XLA Modules:
  0.0 276.9 jit_solution(5832122592408861304)
XLA Ops:
  1.3 272.3 %shard_map.102 = (bf16[3584,1024]{1,0:T(8,128)(2,1)S(1)}, bf16[8,28]{1,0:T(8,128)(2,1)S(1)}, bf16[128,1024]{1,0:T(8,128)(2,1)S(1)}, s32[1,3]{1,0:T(1,128)S(1)}) custom-call(bf16[2,3584,1024]{2,1,0:T(8,128)(2,1)} %q.1, bf16[2,8,28]{2,1,0:T(8,128)(2,1)} %bitcast.9, s32[1]{0:T(128)S(6)} %copy.11.place, bf16[16,3584]{1,0:T(8,128)(2,1)} %tokens.1, ...), custom_call_target="tpu_custom_call" | custom-call | tf_op jit(solution)/shard_map/pallas_call | solution.py:542
  273.6 3.1 %shard_map.103 = (bf16[3584,1024]{1,0:T(8,128)(2,1)}, bf16[8,28]{1,0:T(8,128)(2,1)}, bf16[128,1024]{1,0:T(8,128)(2,1)}, s32[1,3]{1,0:T(1,128)}) custom-call(bf16[3584,1024]{1,0:T(8,128)(2,1)S(1)} %get-tuple-element.12.w, bf16[8,28]{1,0:T(8,128)(2,1)S(1)} %get-tuple-element.13.scale, bf16[128,1024]{1,0:T(8,128)(2,1)S(1)} %get-tuple-element.14.hidden, ...), custom_call_target="tpu_custom_call" | custom-call | tf_op jit(solution)/shard_map/pallas_call | solution.py:565
